TPU v7x, 32 devices: a whole 2x2x4 slice. The times are simulated.
32 devices in a mesh: dp: 8 (over z, core), ctx: 4 (over y, x).
Axes of the slice: x: 2, y: 2, z: 4, core: 2. Of those that a mesh axis runs over, the one named last changes fastest.
Arguments:
- block_input: float32 [8, 512, 1088], P('dp', 'ctx'), may hold values from -6 to 6
- block_pairs: int32 [4], replicated, may hold values from 0 to 3, each once
- attend_gain: bfloat16 [1088], P('dp'), may hold values from 0.5 to 1.5
- attend_shift: bfloat16 [1088], P('dp'), may hold values from -3 to 3
- input_weight: bfloat16 [1088, 3264], P('dp', 'ctx'), may hold values from -1 to 1
- query_bias: bfloat16 [1088], P('dp'), may hold values from -3 to 3
- value_bias: bfloat16 [1088], P('dp'), may hold values from -3 to 3
- output_weight: bfloat16 [1088, 1088], P('dp', 'ctx'), may hold values from -1.5 to 1.5
- output_bias: bfloat16 [1088], P('dp'), may hold values from -3 to 3
- feed_gain: bfloat16 [1088], P('dp'), may hold values from 0.5 to 1.5
- feed_shift: bfloat16 [1088], P('dp'), may hold values from -3 to 3
- expand_weight: bfloat16 [1088, 4352], P('dp', 'ctx'), may hold values from -0.1875 to 0.1875
- expand_bias: bfloat16 [4352], P('dp'), may hold values from -3 to 3
- reduce_weight: bfloat16 [4352, 1088], P('dp', 'ctx'), may hold values from -0.09375 to 0.09375
- reduce_bias: bfloat16 [1088], P('dp'), may hold values from -3 to 3
- output_cotangent: float32 [8, 512, 1088], P('dp', 'ctx'), may hold values from -6 to 6
Outputs:
- block_output: float32 [8, 512, 1088], P('dp', 'ctx')
- input_grad: float32 [8, 512, 1088], P('dp', 'ctx')
- grad_attend_gain: float32 [1088], P('dp')
- grad_attend_shift: float32 [1088], P('dp')
- grad_input_weight: float32 [1088, 3264], P('dp', 'ctx')
- grad_query_bias: float32 [1088], P('dp')
- grad_value_bias: float32 [1088], P('dp')
- grad_output_weight: float32 [1088, 1088], P('dp', 'ctx')
- grad_output_bias: float32 [1088], P('dp')
- grad_feed_gain: float32 [1088], P('dp')
- grad_feed_shift: float32 [1088], P('dp')
- grad_expand_weight: float32 [1088, 4352], P('dp', 'ctx')
- grad_expand_bias: float32 [4352], P('dp')
- grad_reduce_weight: float32 [4352, 1088], P('dp', 'ctx')
- grad_reduce_bias: float32 [1088], P('dp')
Inputs may be any that keep to these rules, and one draw needn't show every extreme that they name: `block_pairs`: each number from 0 to 3 appears once.
All inputs are finite; a program needn't handle non-finite values.
Results may differ from a plain program's by a relative error of at most 0.012.
The roundings to bfloat16 on the way count: a program that leaves them out, or rounds other values in their place, can miss the bound.
Values may be sent and summed in bfloat16 or wider, within the bound.
No kernel may reach another device: no remote copies, remote signals or barrier semaphores. Data moves between devices by JAX's collectives and lax.ppermute only.
A program may use at most 256 MiB of HBM per device.

v0:
```python
import jax
import jax.numpy as jnp
from jax import lax
from jax.sharding import PartitionSpec as P

HEADS = 17
HEAD_DIM = 64


EPSILON = 1e-05
GELU_ROOT = 0.7978845608028654
GELU_CUBIC = 0.044715
MASKED = -1e30


def layer_norm(matrix, norm_gain, norm_shift):
    average = jnp.mean(matrix, axis=-1, keepdims=True)
    centered = matrix - average
    variance = jnp.mean(centered * centered, axis=-1, keepdims=True)
    inverse = lax.rsqrt(variance + EPSILON)
    normed = centered * inverse
    return (
        normed * norm_gain.astype(jnp.float32) + norm_shift.astype(jnp.float32),
        normed,
        inverse,
    )


def norm_backward(upstream, normed, inverse, norm_gain):
    grad_gain = jnp.sum(upstream * normed, axis=0)
    grad_shift = jnp.sum(upstream, axis=0)
    scaled = upstream * norm_gain.astype(jnp.float32)
    centred_grad = (
        scaled
        - jnp.mean(scaled, axis=-1, keepdims=True)
        - normed * jnp.mean(scaled * normed, axis=-1, keepdims=True)
    )
    return (inverse * centred_grad, grad_gain, grad_shift)


def gelu_pair(before):
    cubic = GELU_ROOT * (before + GELU_CUBIC * before * before * before)
    tangent = jnp.tanh(cubic)
    result = 0.5 * before * (1.0 + tangent)
    derivative = 0.5 * (1.0 + tangent) + 0.5 * before * (1.0 - tangent * tangent) * GELU_ROOT * (
        1.0 + 3.0 * GELU_CUBIC * before * before
    )
    return (result, derivative)


def split_heads(matrix):
    return matrix.reshape(matrix.shape[:-1] + (HEADS, HEAD_DIM))


def pick_halves(slots_all, early_flag, half_rows):
    pair_count = early_flag.shape[0]
    width = slots_all.shape[-1]
    slot_view = slots_all.reshape(pair_count, 2, half_rows, width)
    chosen = jnp.where(early_flag[:, None, None], slot_view[:, 0], slot_view[:, 1])
    early_all = slot_view[:, 0].reshape(pair_count * half_rows, width)
    return (chosen, early_all)


def pair_scores(queries, keys_all, keys_local, early_flag, own_mask):
    half_rows = queries.shape[0] // 2
    scale = HEAD_DIM ** (-0.5)
    query_early = queries[:half_rows]
    query_late = queries[half_rows:]
    query_pick = jnp.where(early_flag[:, None, None], query_early[None], query_late[None])
    key_pick, key_early = pick_halves(keys_all, early_flag, half_rows)
    key_own = keys_local[half_rows:]
    causal = jnp.arange(half_rows)[None, :] <= jnp.arange(half_rows)[:, None]
    score_full = (
        jnp.einsum(
            "rhe,lhe->hrl",
            split_heads(query_late),
            split_heads(key_early),
            preferred_element_type=jnp.float32,
        )
        * scale
    )
    score_pick = (
        jnp.einsum(
            "crhe,clhe->hrcl",
            split_heads(query_pick),
            split_heads(key_pick),
            preferred_element_type=jnp.float32,
        )
        * scale
    )
    blocked = own_mask[None, None, :, None] & jnp.logical_not(causal)[None, :, None, :]
    score_pick = jnp.where(blocked, MASKED, score_pick)
    score_diag = (
        jnp.einsum(
            "rhe,lhe->hrl",
            split_heads(query_late),
            split_heads(key_own),
            preferred_element_type=jnp.float32,
        )
        * scale
    )
    score_diag = jnp.where(causal[None], score_diag, MASKED)
    return (score_full, score_pick, score_diag, query_pick, key_pick, key_early, key_own)


def pair_exact(score_full, score_pick, score_diag, log_early, log_late, flag):
    log_pick = jnp.where(flag, log_early[:, :, None], log_late[:, :, None])
    return (
        jnp.exp(score_full - log_late[:, :, None]),
        jnp.exp(score_pick - log_pick[:, :, :, None]),
        jnp.exp(score_diag - log_late[:, :, None]),
    )


def pair_forward(queries, keys_all, values_all, keys_local, values_local, early_flag, own_mask):
    half_rows = queries.shape[0] // 2
    width = queries.shape[1]
    score_full, score_pick, score_diag = pair_scores(
        queries, keys_all, keys_local, early_flag, own_mask
    )[:3]
    value_pick, value_early = pick_halves(values_all, early_flag, half_rows)
    flag = early_flag[None, None, :]
    pick_top = jnp.max(score_pick, axis=-1)
    top_early = jnp.max(jnp.where(flag, pick_top, MASKED), axis=-1)
    top_late = jnp.maximum(
        jnp.maximum(jnp.max(score_full, axis=-1), jnp.max(score_diag, axis=-1)),
        jnp.max(jnp.where(flag, MASKED, pick_top), axis=-1),
    )
    top_pick = jnp.where(flag, top_early[:, :, None], top_late[:, :, None])
    pick_sums = jnp.sum(jnp.exp(score_pick - top_pick[:, :, :, None]), axis=-1)
    sum_early = jnp.sum(jnp.where(flag, pick_sums, 0.0), axis=-1)
    sum_late = (
        jnp.sum(jnp.exp(score_full - top_late[:, :, None]), axis=-1)
        + jnp.sum(jnp.exp(score_diag - top_late[:, :, None]), axis=-1)
        + jnp.sum(jnp.where(flag, 0.0, pick_sums), axis=-1)
    )
    log_early = top_early + jnp.log(sum_early)
    log_late = top_late + jnp.log(sum_late)
    exact_full, exact_pick, exact_diag = pair_exact(
        score_full, score_pick, score_diag, log_early, log_late, flag
    )
    flag_rows = early_flag[:, None, None, None]
    out_pick = jnp.einsum(
        "hrcl,clhe->crhe",
        exact_pick.astype(jnp.bfloat16),
        split_heads(value_pick),
        preferred_element_type=jnp.float32,
    )
    early_out = jnp.sum(jnp.where(flag_rows, out_pick, 0.0), axis=0)
    late_out = (
        jnp.sum(jnp.where(flag_rows, 0.0, out_pick), axis=0)
        + jnp.einsum(
            "hrl,lhe->rhe",
            exact_full.astype(jnp.bfloat16),
            split_heads(value_early),
            preferred_element_type=jnp.float32,
        )
        + jnp.einsum(
            "hrl,lhe->rhe",
            exact_diag.astype(jnp.bfloat16),
            split_heads(values_local[half_rows:]),
            preferred_element_type=jnp.float32,
        )
    )
    mixed = (
        jnp.concatenate([early_out, late_out], axis=0)
        .reshape(2 * half_rows, width)
        .astype(jnp.bfloat16)
    )
    return (mixed, log_early, log_late)


def pair_backward(
    queries,
    keys_all,
    values_all,
    keys_local,
    values_local,
    early_flag,
    own_mask,
    log_early,
    log_late,
    mixed,
    grad_mixed,
):
    half_rows = queries.shape[0] // 2
    width = queries.shape[1]
    pair_count = early_flag.shape[0]
    scale = HEAD_DIM ** (-0.5)
    score_full, score_pick, score_diag, query_pick, key_pick, key_early, key_own = pair_scores(
        queries, keys_all, keys_local, early_flag, own_mask
    )
    value_pick, value_early = pick_halves(values_all, early_flag, half_rows)
    value_own = values_local[half_rows:]
    query_late = queries[half_rows:]
    flag = early_flag[None, None, :]
    exact_full, exact_pick, exact_diag = pair_exact(
        score_full, score_pick, score_diag, log_early, log_late, flag
    )
    grad_early = grad_mixed[:half_rows]
    grad_late = grad_mixed[half_rows:]
    delta_early = jnp.einsum(
        "rhe,rhe->hr",
        split_heads(grad_early).astype(jnp.float32),
        split_heads(mixed[:half_rows]).astype(jnp.float32),
    )
    delta_late = jnp.einsum(
        "rhe,rhe->hr",
        split_heads(grad_late).astype(jnp.float32),
        split_heads(mixed[half_rows:]).astype(jnp.float32),
    )
    grad_pick = jnp.where(early_flag[:, None, None], grad_early[None], grad_late[None])
    delta_pick = jnp.where(flag, delta_early[:, :, None], delta_late[:, :, None])
    dprob_pick = jnp.einsum(
        "crhe,clhe->hrcl",
        split_heads(grad_pick),
        split_heads(value_pick),
        preferred_element_type=jnp.float32,
    )
    dscore_pick = (exact_pick * (dprob_pick - delta_pick[:, :, :, None]) * scale).astype(
        jnp.bfloat16
    )
    dvalue_pick = jnp.einsum(
        "hrcl,crhe->clhe",
        exact_pick.astype(jnp.bfloat16),
        split_heads(grad_pick),
        preferred_element_type=jnp.float32,
    )
    dkey_pick = jnp.einsum(
        "hrcl,crhe->clhe", dscore_pick, split_heads(query_pick), preferred_element_type=jnp.float32
    )
    dquery_pick = jnp.einsum(
        "hrcl,clhe->crhe", dscore_pick, split_heads(key_pick), preferred_element_type=jnp.float32
    )
    dprob_full = jnp.einsum(
        "rhe,lhe->hrl",
        split_heads(grad_late),
        split_heads(value_early),
        preferred_element_type=jnp.float32,
    )
    dscore_full = (exact_full * (dprob_full - delta_late[:, :, None]) * scale).astype(jnp.bfloat16)
    dvalue_early = jnp.einsum(
        "hrl,rhe->lhe",
        exact_full.astype(jnp.bfloat16),
        split_heads(grad_late),
        preferred_element_type=jnp.float32,
    )
    dkey_early = jnp.einsum(
        "hrl,rhe->lhe", dscore_full, split_heads(query_late), preferred_element_type=jnp.float32
    )
    dquery_full = jnp.einsum(
        "hrl,lhe->rhe", dscore_full, split_heads(key_early), preferred_element_type=jnp.float32
    )
    dprob_diag = jnp.einsum(
        "rhe,lhe->hrl",
        split_heads(grad_late),
        split_heads(value_own),
        preferred_element_type=jnp.float32,
    )
    dscore_diag = (exact_diag * (dprob_diag - delta_late[:, :, None]) * scale).astype(jnp.bfloat16)
    dvalue_diag = jnp.einsum(
        "hrl,rhe->lhe",
        exact_diag.astype(jnp.bfloat16),
        split_heads(grad_late),
        preferred_element_type=jnp.float32,
    )
    dkey_diag = jnp.einsum(
        "hrl,rhe->lhe", dscore_diag, split_heads(query_late), preferred_element_type=jnp.float32
    )
    dquery_diag = jnp.einsum(
        "hrl,lhe->rhe", dscore_diag, split_heads(key_own), preferred_element_type=jnp.float32
    )
    flag_slots = early_flag[:, None, None]
    flag_rows = early_flag[:, None, None, None]

    def assemble(early_part, pick_part):
        pick_flat = pick_part.reshape(pair_count, half_rows, width)
        first = early_part.reshape(pair_count, half_rows, width) + jnp.where(
            flag_slots, pick_flat, 0.0
        )
        second = jnp.where(flag_slots, 0.0, pick_flat)
        return jnp.stack([first, second], axis=1).reshape(pair_count * 2 * half_rows, width)

    key_grads = assemble(dkey_early, dkey_pick)
    value_grads = assemble(dvalue_early, dvalue_pick)
    query_first = jnp.sum(jnp.where(flag_rows, dquery_pick, 0.0), axis=0)
    query_second = (
        jnp.sum(jnp.where(flag_rows, 0.0, dquery_pick), axis=0) + dquery_full + dquery_diag
    )
    grad_queries = jnp.concatenate([query_first, query_second], axis=0).reshape(
        2 * half_rows, width
    )
    return (
        grad_queries,
        key_grads,
        value_grads,
        dkey_diag.reshape(half_rows, width),
        dvalue_diag.reshape(half_rows, width),
    )


def body(
    block_input,
    block_pairs,
    attend_gain,
    attend_shift,
    input_weight,
    query_bias,
    value_bias,
    output_weight,
    output_bias,
    feed_gain,
    feed_shift,
    expand_weight,
    expand_bias,
    reduce_weight,
    reduce_bias,
    output_cotangent,
):
    inputs = block_input[0]
    cotangent = output_cotangent[0]
    local_rows = inputs.shape[0]
    model_width = inputs.shape[1]
    half_rows = local_rows // 2
    pair_count = lax.axis_size("ctx")
    slot_ids = jnp.arange(pair_count, dtype=jnp.int32)
    own_mask = slot_ids == lax.axis_index("ctx")
    my_pair = jnp.sum(jnp.where(own_mask, block_pairs, 0))
    early_flag = block_pairs <= my_pair
    matrix_cols = (
        lax.all_gather(input_weight, "ctx", axis=1, tiled=True),
        lax.all_gather(output_weight, "ctx", axis=1, tiled=True),
        lax.all_gather(expand_weight, "ctx", axis=1, tiled=True),
        lax.all_gather(reduce_weight, "ctx", axis=1, tiled=True),
    )
    attend_set = (
        lax.all_gather(attend_gain, "dp", axis=0, tiled=True),
        lax.all_gather(attend_shift, "dp", axis=0, tiled=True),
        lax.all_gather(matrix_cols[0], "dp", axis=0, tiled=True),
        lax.all_gather(query_bias, "dp", axis=0, tiled=True),
        lax.all_gather(value_bias, "dp", axis=0, tiled=True),
        lax.all_gather(matrix_cols[1], "dp", axis=0, tiled=True),
        lax.all_gather(output_bias, "dp", axis=0, tiled=True),
    )
    (
        full_attend_gain,
        full_attend_shift,
        full_input_weight,
        full_query_bias,
        full_value_bias,
        full_output_weight,
        full_output_bias,
    ) = attend_set
    normed_in, first_normed, first_inverse = layer_norm(inputs, full_attend_gain, full_attend_shift)
    attend_in = normed_in.astype(jnp.bfloat16)
    projected = jnp.dot(attend_in, full_input_weight, preferred_element_type=jnp.float32)
    queries = (projected[:, :model_width] + full_query_bias.astype(jnp.float32)).astype(
        jnp.bfloat16
    )
    keys = projected[:, model_width : 2 * model_width].astype(jnp.bfloat16)
    values = (projected[:, 2 * model_width :] + full_value_bias.astype(jnp.float32)).astype(
        jnp.bfloat16
    )
    keys_all, values_all = (
        lax.all_gather(keys, "ctx", axis=0, tiled=True),
        lax.all_gather(values, "ctx", axis=0, tiled=True),
    )
    mixed, log_early, log_late = pair_forward(
        queries, keys_all, values_all, keys, values, early_flag, own_mask
    )
    resid = (
        inputs
        + jnp.dot(mixed, full_output_weight, preferred_element_type=jnp.float32)
        + full_output_bias.astype(jnp.float32)
    )
    feed_set = (
        lax.all_gather(feed_gain, "dp", axis=0, tiled=True),
        lax.all_gather(feed_shift, "dp", axis=0, tiled=True),
        lax.all_gather(matrix_cols[2], "dp", axis=0, tiled=True),
        lax.all_gather(expand_bias, "dp", axis=0, tiled=True),
        lax.all_gather(matrix_cols[3], "dp", axis=0, tiled=True),
        lax.all_gather(reduce_bias, "dp", axis=0, tiled=True),
    )
    (
        full_feed_gain,
        full_feed_shift,
        full_expand_weight,
        full_expand_bias,
        full_reduce_weight,
        full_reduce_bias,
    ) = feed_set
    normed_mid, second_normed, second_inverse = layer_norm(resid, full_feed_gain, full_feed_shift)
    feed_in = normed_mid.astype(jnp.bfloat16)
    before = jnp.dot(
        feed_in, full_expand_weight, preferred_element_type=jnp.float32
    ) + full_expand_bias.astype(jnp.float32)
    activated, slope = gelu_pair(before)
    activ_low = activated.astype(jnp.bfloat16)
    output = (
        resid
        + jnp.dot(activ_low, full_reduce_weight, preferred_element_type=jnp.float32)
        + full_reduce_bias.astype(jnp.float32)
    )
    back_feed_gain = feed_set[0]
    back_expand_weight = feed_set[2]
    back_reduce_weight = feed_set[4]
    cot_low = cotangent.astype(jnp.bfloat16)
    grad_reduce_bias = jnp.sum(cotangent, axis=0)
    grad_before = jnp.dot(cot_low, back_reduce_weight.T, preferred_element_type=jnp.float32) * slope
    before_low = grad_before.astype(jnp.bfloat16)
    grad_expand_bias = jnp.sum(grad_before, axis=0)
    grad_feed_in = jnp.dot(before_low, back_expand_weight.T, preferred_element_type=jnp.float32)
    grad_mid, grad_feed_gain, grad_feed_shift = norm_backward(
        grad_feed_in, second_normed, second_inverse, back_feed_gain
    )
    rows_all = (
        lax.all_gather(attend_in, "ctx", axis=0, tiled=True),
        lax.all_gather(mixed, "ctx", axis=0, tiled=True),
        lax.all_gather(feed_in, "ctx", axis=0, tiled=True),
        lax.all_gather(activ_low, "ctx", axis=0, tiled=True),
    )
    cot_share, before_share = (
        lax.all_to_all(cot_low, "ctx", split_axis=1, concat_axis=0, tiled=True),
        lax.all_to_all(before_low, "ctx", split_axis=1, concat_axis=0, tiled=True),
    )
    share_reduce = jnp.dot(rows_all[3].T, cot_share, preferred_element_type=jnp.float32)
    share_expand = jnp.dot(rows_all[2].T, before_share, preferred_element_type=jnp.float32)
    back_attend_gain = attend_set[0]
    back_input_weight = attend_set[2]
    back_output_weight = attend_set[5]
    grad_resid = cotangent + grad_mid
    resid_low = grad_resid.astype(jnp.bfloat16)
    grad_output_bias = jnp.sum(grad_resid, axis=0)
    grad_mixed = jnp.dot(
        resid_low, back_output_weight.T, preferred_element_type=jnp.float32
    ).astype(jnp.bfloat16)
    grad_queries, grad_keys_all, grad_values_all, own_key_grad, own_value_grad = pair_backward(
        queries,
        keys_all,
        values_all,
        keys,
        values,
        early_flag,
        own_mask,
        log_early,
        log_late,
        mixed,
        grad_mixed,
    )
    summed_keys, summed_values = (
        lax.psum_scatter(grad_keys_all, "ctx", scatter_dimension=0, tiled=True),
        lax.psum_scatter(grad_values_all, "ctx", scatter_dimension=0, tiled=True),
    )
    grad_keys = jnp.concatenate(
        [summed_keys[:half_rows], summed_keys[half_rows:] + own_key_grad], axis=0
    )
    grad_values = jnp.concatenate(
        [summed_values[:half_rows], summed_values[half_rows:] + own_value_grad], axis=0
    )
    grad_query_bias = jnp.sum(grad_queries, axis=0)
    grad_value_bias = jnp.sum(grad_values, axis=0)
    grad_proj = jnp.concatenate([grad_queries, grad_keys, grad_values], axis=1).astype(jnp.bfloat16)
    grad_attend_in = jnp.dot(grad_proj, back_input_weight.T, preferred_element_type=jnp.float32)
    grad_first, grad_attend_gain, grad_attend_shift = norm_backward(
        grad_attend_in, first_normed, first_inverse, back_attend_gain
    )
    input_grad = grad_resid + grad_first
    resid_share, proj_share = (
        lax.all_to_all(resid_low, "ctx", split_axis=1, concat_axis=0, tiled=True),
        lax.all_to_all(grad_proj, "ctx", split_axis=1, concat_axis=0, tiled=True),
    )
    share_input = jnp.dot(rows_all[0].T, proj_share, preferred_element_type=jnp.float32)
    share_output = jnp.dot(rows_all[1].T, resid_share, preferred_element_type=jnp.float32)
    row_parts = (
        lax.psum_scatter(share_input, "dp", scatter_dimension=0, tiled=True),
        lax.psum_scatter(share_output, "dp", scatter_dimension=0, tiled=True),
        lax.psum_scatter(share_expand, "dp", scatter_dimension=0, tiled=True),
        lax.psum_scatter(share_reduce, "dp", scatter_dimension=0, tiled=True),
        lax.psum_scatter(grad_attend_gain, "dp", scatter_dimension=0, tiled=True),
        lax.psum_scatter(grad_attend_shift, "dp", scatter_dimension=0, tiled=True),
        lax.psum_scatter(grad_query_bias, "dp", scatter_dimension=0, tiled=True),
        lax.psum_scatter(grad_value_bias, "dp", scatter_dimension=0, tiled=True),
        lax.psum_scatter(grad_output_bias, "dp", scatter_dimension=0, tiled=True),
        lax.psum_scatter(grad_feed_gain, "dp", scatter_dimension=0, tiled=True),
        lax.psum_scatter(grad_feed_shift, "dp", scatter_dimension=0, tiled=True),
        lax.psum_scatter(grad_expand_bias, "dp", scatter_dimension=0, tiled=True),
        lax.psum_scatter(grad_reduce_bias, "dp", scatter_dimension=0, tiled=True),
    )
    (
        shard_attend_gain,
        shard_attend_shift,
        shard_query_bias,
        shard_value_bias,
        shard_output_bias,
        shard_feed_gain,
        shard_feed_shift,
        shard_expand_bias,
        shard_reduce_bias,
    ) = lax.psum(
        (
            row_parts[4],
            row_parts[5],
            row_parts[6],
            row_parts[7],
            row_parts[8],
            row_parts[9],
            row_parts[10],
            row_parts[11],
            row_parts[12],
        ),
        "ctx",
    )
    return (
        output[None],
        input_grad[None],
        shard_attend_gain,
        shard_attend_shift,
        row_parts[0],
        shard_query_bias,
        shard_value_bias,
        row_parts[1],
        shard_output_bias,
        shard_feed_gain,
        shard_feed_shift,
        row_parts[2],
        shard_expand_bias,
        row_parts[3],
        shard_reduce_bias,
    )


def solution(mesh):
    placed = (
        P("dp", "ctx", None),
        P(),
        P("dp"),
        P("dp"),
        P("dp", "ctx"),
        P("dp"),
        P("dp"),
        P("dp", "ctx"),
        P("dp"),
        P("dp"),
        P("dp"),
        P("dp", "ctx"),
        P("dp"),
        P("dp", "ctx"),
        P("dp"),
        P("dp", "ctx", None),
    )
    return jax.shard_map(
        body,
        mesh=mesh,
        in_specs=placed,
        out_specs=(
            P("dp", "ctx", None),
            P("dp", "ctx", None),
            P("dp"),
            P("dp"),
            P("dp", "ctx"),
            P("dp"),
            P("dp"),
            P("dp", "ctx"),
            P("dp"),
            P("dp"),
            P("dp"),
            P("dp", "ctx"),
            P("dp"),
            P("dp", "ctx"),
            P("dp"),
        ),
        check_vma=False,
    )
```

profile of v0, /device:TPU:0, one launch (start us, length us, event | category | flops | bytes accessed | tf_op | source)
XLA Modules:
  0.0 906.0 jit_solution(594871689538817184)
XLA Ops:
  7.2 15.4 %all-gather = bf16[4,816,136]{1,2,0:T(8,128)(2,1)S(1)} all-gather(bf16[1,816,136]{1,2,0:T(8,128)(2,1)} %bitcast.246), channel_id=1, replica_groups=mesh['dp'=8,'ctx'=4] {'ctx'}, dimensions={0}, use_global_device_ids=true | all-gather | bytes 1109760 | tf_op jit(solution)/shard_map/all_gather | solution.py:331
  23.2 1.7 reshape.364
  30.6 30.9 %all-reduce.23 = (bf16[1088]{0:T(1024)(128)(2,1)S(1)}, bf16[1088]{0:T(1024)(128)(2,1)S(1)}, bf16[1088]{0:T(1024)(128)(2,1)S(1)}, bf16[1088]{0:T(1024)(128)(2,1)S...) all-reduce(bf16[1088]{0:T(1024)(128)(2,1)S(1)} %dynamic-update-slic, ...), channel_id=1, replica_groups=mesh['dp'=8,'ctx'=4] {'dp'}, use_global_device_ids=true, to_apply=%add.1 | all-reduce | flops 13056 | bytes 52224
  62.2 36.5 %all-gather.16.cloned.1.call-done = bf16[1088,3264]{1,0:T(8,128)(2,1)} async-done(((bf16[136,3264]{1,0:T(8,128)(2,1)}), bf16[1088,3264]{1,0:T(8,128)(2,1)}) %all-gather.16.cloned.1.call-update) | async-done | bytes 7102480 | tf_op jit(solution)/shard_map/all_gather | solution.py:339
  98.7 6.0 fusion.69
  106.7 11.1 %all-gather.1 = bf16[4,272,136]{1,2,0:T(8,128)(2,1)S(1)} all-gather(bf16[1,272,136]{1,2,0:T(8,128)(2,1)S(1)} %bitcast.247), channel_id=1, replica_groups=mesh['dp'=8,'ctx'=4] {'ctx'}, dimensions={0}, use_global_device_ids=true | all-gather | bytes 369920 | tf_op jit(solution)/shard_map/all_gather | solution.py:332
  119.0 10.2 %all-gather.38.cloned.1.call-done = bf16[4,1088,136]{1,2,0:T(8,128)(2,1)} async-done(((bf16[1,1088,136]{1,2,0:T(8,128)(2,1)}), bf16[4,1088,136]{1,2,0:T(8,128)(2,1)}) %all-gather.38.cloned.1.call-update) | async-done | bytes 1183760 | tf_op jit(solution)/shard_map/all_gather | solution.py:333
  129.3 1.8 copy.224
  131.1 2.0 reshape.368
  133.1 27.4 %all-gather.26.cloned.1.call-done = bf16[544,1088]{0,1:T(8,128)(2,1)} async-done(((bf16[544,272]{0,1:T(8,128)(2,1)}), bf16[544,1088]{0,1:T(8,128)(2,1)}) %all-gather.26.cloned.1.call-update) | async-done | bytes 1183760 | tf_op jit(solution)/shard_map/all_gather | solution.py:334
  160.5 2.6 copy.225
  166.7 22.9 %all-gather.20.cloned.1.call-done = bf16[512,1088]{0,1:T(8,128)(2,1)} async-done(((bf16[128,1088]{0,1:T(8,128)(2,1)}), bf16[512,1088]{0,1:T(8,128)(2,1)}) %all-gather.20.cloned.1.call-update) | async-done | bytes 1114128 | tf_op jit(solution)/shard_map/all_gather | solution.py:365
  189.7 1.9 copy.211
  193.8 1.9 copy.216
  195.8 23.1 %all-gather.18.cloned.1.call-done = bf16[512,1088]{0,1:T(8,128)(2,1)} async-done(((bf16[128,1088]{0,1:T(8,128)(2,1)}), bf16[512,1088]{0,1:T(8,128)(2,1)}) %all-gather.18.cloned.1.call-update) | async-done | bytes 1114128 | tf_op jit(solution)/shard_map/all_gather | solution.py:366
  218.9 1.7 copy.208
  222.8 2.0 copy.221
  224.8 2.3 copy.210
  229.2 3.0 reshape_reshape_squeeze.10
  232.2 2.4 broadcast_select_fusion.3
  240.3 13.3 %all-gather.22.cloned.1.call-done = bf16[1088,1088]{1,0:T(8,128)(2,1)} async-done(((bf16[136,1088]{1,0:T(8,128)(2,1)}), bf16[1088,1088]{1,0:T(8,128)(2,1)}) %all-gather.22.cloned.1.call-update) | async-done | bytes 2367504 | tf_op jit(solution)/shard_map/all_gather | solution.py:342
  253.7 2.9 fusion.73
  257.1 88.4 %all-gather.24.cloned.1.call-done = bf16[1088,4352]{1,0:T(8,128)(2,1)} async-done(((bf16[136,4352]{1,0:T(8,128)(2,1)}), bf16[1088,4352]{1,0:T(8,128)(2,1)}) %all-gather.24.cloned.1.call-update) | async-done | bytes 9469968 | tf_op jit(solution)/shard_map/all_gather | solution.py:379
  345.5 7.6 multiply_convert_fusion
  355.0 86.2 %all-gather.28.cloned.1.call-done = bf16[4352,1088]{1,0:T(8,128)(2,1)} async-done(((bf16[544,1088]{1,0:T(8,128)(2,1)}), bf16[4352,1088]{1,0:T(8,128)(2,1)}) %all-gather.28.cloned.1.call-update) | async-done | bytes 9469968 | tf_op jit(solution)/shard_map/all_gather | solution.py:381
  441.2 7.7 fusion.61
  448.9 2.8 multiply_reduce_fusion
  453.7 1.8 convolution_convert_fusion
  458.3 2.0 fusion.10
  461.6 3.2 reshape.328
  464.9 2.4 reshape.332
  467.3 2.2 fusion.28
  472.4 7.9 select_add_fusion
  480.3 2.7 pad_maximum_fusion.1
  483.0 5.7 copy.246
  488.8 4.3 pad_maximum_fusion
  493.1 5.7 copy.240
  500.1 12.5 %all_to_all.70 = bf16[128,4,272]{0,2,1:T(8,128)(2,1)S(1)} all-to-all(bf16[128,4,272]{0,2,1:T(8,128)(2,1)S(1)} %bitcast.242), channel_id=1, replica_groups=mesh['dp'=8,'ctx'=4] {'ctx'}, dimensions={1} | all-to-all | bytes 557056 | tf_op jit(solution)/shard_map/all_to_all | solution.py:423
  512.6 7.5 fusion.45
  520.1 3.5 all-to-all-start.1
  523.9 2.3 all-gather.32.cloned.1.call-done
  526.2 2.8 all-to-all-done.1
  529.0 3.2 fusion.48
  532.2 1.5 copy.253
  533.7 20.1 %all_to_all.71 = bf16[128,4,1088]{0,2,1:T(8,128)(2,1)} all-to-all(bf16[128,4,1088]{0,2,1:T(8,128)(2,1)} %bitcast.219), channel_id=1, replica_groups=mesh['dp'=8,'ctx'=4] {'ctx'}, dimensions={1} | all-to-all | bytes 2228224 | tf_op jit(solution)/shard_map/all_to_all | solution.py:424
  553.8 1.7 copy.254
  555.5 7.1 all-gather.34.cloned.1.call-done
  562.5 5.1 fusion.79
  569.6 2.5 select_reduce_fusion.3
  572.9 29.9 %reduce-scatter.17.cloned.1.call-done = f32[128,1088]{1,0:T(8,128)} async-done(((f32[512,1088]{1,0:T(8,128)}), f32[128,1088]{1,0:T(8,128)}) %reduce-scatter.17.cloned.1.call-update) | async-done | bytes 557072 | tf_op jit(solution)/shard_map/reduce_scatter | solution.py:452
  605.0 38.3 %reduce-scatter.15.cloned.1.call-done = f32[128,1088]{1,0:T(8,128)} async-done(((f32[512,1088]{1,0:T(8,128)}), f32[128,1088]{1,0:T(8,128)}) %reduce-scatter.15.cloned.1.call-update) | async-done | bytes 557072 | tf_op jit(solution)/shard_map/reduce_scatter | solution.py:451
  646.2 3.5 all-to-all-start
  649.7 28.0 %all-gather.30.cloned.1.call-done = bf16[512,1088]{0,1:T(8,128)(2,1)} async-done(((bf16[128,1088]{0,1:T(8,128)(2,1)}), bf16[512,1088]{0,1:T(8,128)(2,1)}) %all-gather.30.cloned.1.call-update) | async-done | bytes 1114128 | tf_op jit(solution)/shard_map/all_gather | solution.py:417
  677.7 4.5 fusion.36
  684.0 8.8 fusion.2
  692.8 2.9 multiply_reduce_fusion.1
  695.7 32.5 %all-reduce.21 = (f32[1088]{0:T(1024)S(1)}, f32[1088]{0:T(1024)S(1)}, f32[1088]{0:T(1024)S(1)}, f32[1088]{0:T(1024)S(1)}, f32[1088]{0:T(1024)S(1)}, /*index=5*/f...) all-reduce(f32[1088]{0:T(1024)S(1)} %get-tuple-element.22, ...), channel_id=4, replica_groups=mesh['dp'=8,'ctx'=4] {'dp'}, use_global_device_ids=true, to_apply=%region_26.27.clone | all-reduce | flops 13056 | bytes 104448
  728.9 15.7 %all-reduce.22 = (f32[136]{0:T(256)}, f32[136]{0:T(256)}, f32[136]{0:T(256)}, f32[136]{0:T(256)}, f32[136]{0:T(256)}, /*index=5*/f32[136]{0:T(256)}, f32[136]{0:T(256)}, f32[544]{0:T(1024)}, f32[136]{0:T(256)}) all-reduce(f32[136]{0:T(256)S(1)} %dynamic-slice.10, ...), channel_id=1, replica_groups=mesh['dp'=8,'ctx'=4] {'ctx'}, use_global_device_ids=true, to_apply=%region_27.28 | all-reduce | flops 1632 | bytes 13056 | tf_op jit(solution)/shard_map/psum | solution.py:499
  744.6 2.4 add_bitcast_fusion
  747.0 8.2 reduce-scatter.19.cloned.1.call-done
  755.2 2.3 copy.300
  757.5 33.6 %reduce-scatter.23.cloned.1.call-done = f32[136,272]{1,0:T(8,128)} async-done(((f32[1088,272]{1,0:T(8,128)}), f32[136,272]{1,0:T(8,128)}) %reduce-scatter.23.cloned.1.call-update) | async-done | bytes 147984
  791.1 59.0 %reduce-scatter.25.cloned.1.call-done = f32[136,1088]{1,0:T(8,128)} async-done(((f32[1088,1088]{1,0:T(8,128)}), f32[136,1088]{1,0:T(8,128)}) %reduce-scatter.25.cloned.1.call-update) | async-done | bytes 591888
  850.1 48.6 %reduce-scatter.21.cloned.1.call-done = f32[136,816]{1,0:T(8,128)} async-done(((f32[1088,816]{1,0:T(8,128)}), f32[136,816]{1,0:T(8,128)}) %reduce-scatter.21.cloned.1.call-update) | async-done | bytes 443920
  (282 shorter events, 45.8 us)
Async XLA Ops:
  7.2 91.6 %all-gather.16.cloned.1.call-start = ((), (), s32[]{:S(2)}) async-start(), calls=%async_computation.10 | async-start | bytes 8146944 | tf_op jit(solution)/shard_map/all_gather | solution.py:339
  23.0 3.4 copy-start.47
  23.0 5.3 copy-start.49
  23.1 5.5 copy-start.50
  23.1 5.8 copy-start.51
  23.1 6.0 copy-start.52
  23.1 6.3 copy-start.53
  23.1 6.5 copy-start.54
  23.1 6.7 copy-start.55
  23.1 7.0 copy-start.56
  23.1 7.2 copy-start.48
  23.1 38.4 %copy-start = (f32[1,128,1088]{1,2,0:T(8,128)S(1)}, f32[1,128,1088]{1,2,0:T(8,128)}, u32[]{:S(2)}) copy-start(f32[1,128,1088]{1,2,0:T(8,128)} %param.16) | copy-start | bytes 1671172
  24.9 104.4 %all-gather.38.cloned.1.call-start = ((), (), s32[]{:S(2)}) async-start(), calls=%async_computation.23 | async-start | bytes 1566720 | tf_op jit(solution)/shard_map/all_gather | solution.py:333
  25.6 134.9 %all-gather.26.cloned.1.call-start = ((), (), s32[]{:S(2)}) async-start(), calls=%async_computation.15 | async-start | bytes 1740800 | tf_op jit(solution)/shard_map/all_gather | solution.py:334
  26.4 163.3 %all-gather.20.cloned.1.call-start = ((), (), s32[]{:S(2)}) async-start(), calls=%async_computation.12 | async-start | bytes 1392640 | tf_op jit(solution)/shard_map/all_gather | solution.py:365
  62.2 42.5 %copy-start.26 = (bf16[128,1088]{0,1:T(8,128)(2,1)}, bf16[128,1088]{0,1:T(8,128)(2,1)S(1)}, u32[]{:S(2)}) copy-start(bf16[128,1088]{0,1:T(8,128)(2,1)S(1)} %add_convert_fusion.1) | copy-start | bytes 835588
  105.5 113.4 %all-gather.18.cloned.1.call-start = ((), (), s32[]{:S(2)}) async-start(), calls=%async_computation.11 | async-start | bytes 1392640 | tf_op jit(solution)/shard_map/all_gather | solution.py:366
  106.6 147.0 %all-gather.22.cloned.1.call-start = ((), (), s32[]{:S(2)}) async-start(), calls=%async_computation.13 | async-start | bytes 2820096 | tf_op jit(solution)/shard_map/all_gather | solution.py:342
  119.0 226.5 %all-gather.24.cloned.1.call-start = ((), (), s32[]{:S(2)}) async-start(), calls=%async_computation.14 | async-start | bytes 10653696 | tf_op jit(solution)/shard_map/all_gather | solution.py:379
  133.0 30.2 %copy-start.57 = (s32[4]{0:T(128)S(1)}, s32[4]{0:T(128)}, u32[]{:S(2)}) copy-start(s32[4]{0:T(128)} %param.17) | copy-start | bytes 52
  133.1 31.7 %copy-start.28 = (bf16[128,1088]{0,1:T(8,128)(2,1)S(1)}, bf16[128,1088]{0,1:T(8,128)(2,1)}, u32[]{:S(2)}) copy-start(bf16[128,1088]{0,1:T(8,128)(2,1)} %get-tuple-element.70) | copy-start | bytes 835588
  133.1 308.1 %all-gather.28.cloned.1.call-start = ((), (), s32[]{:S(2)}) async-start(), calls=%async_computation.16 | async-start | bytes 11280384 | tf_op jit(solution)/shard_map/all_gather | solution.py:381
  163.1 349.5 %all-gather.36.cloned.1.call-start = ((), (), s32[]{:S(2)}) async-start(), calls=%async_computation.22 | async-start | bytes 5570560 | tf_op jit(solution)/shard_map/all_gather | solution.py:420
  164.8 26.8 %copy-start.34 = (bf16[64,1088]{0,1:T(8,128)(2,1)}, bf16[64,1088]{0,1:T(8,128)(2,1)S(1)}, u32[]{:S(2)}) copy-start(bf16[64,1088]{0,1:T(8,128)(2,1)S(1)} %slice.96) | copy-start | bytes 417796
  166.4 69.4 %copy-start.3 = (bf16[64,1088]{0,1:T(8,128)(2,1)}, bf16[64,1088]{0,1:T(8,128)(2,1)S(1)}, u32[]{:S(2)}) copy-start(bf16[64,1088]{0,1:T(8,128)(2,1)S(1)} %get-tuple-element.83) | copy-start | bytes 417796
  221.5 5.7 copy-start.38
  224.8 3.7 copy-start.22
  229.2 6.6 copy-start.16
  229.2 3.1 copy-start.23
  234.7 3.3 copy-start.44
  235.7 2.3 copy-start.7
  240.3 16.4 %copy-start.27 = (bf16[128,17,64]{0,2,1:T(8,128)(2,1)}, bf16[128,17,64]{0,2,1:T(8,128)(2,1)S(1)}, u32[]{:S(2)}) copy-start(bf16[128,17,64]{0,2,1:T(8,128)(2,1)S(1)} %pad_maximum_fusion.5) | copy-start | bytes 835588
  256.5 195.2 %copy-start.2 = (f32[128,1088]{0,1:T(8,128)}, f32[128,1088]{0,1:T(8,128)S(1)}, u32[]{:S(2)}) copy-start(f32[128,1088]{0,1:T(8,128)S(1)} %get-tuple-element.100) | copy-start | bytes 1671172
  257.1 96.1 %copy-start.24 = (bf16[128,1088]{0,1:T(8,128)(2,1)}, bf16[128,1088]{0,1:T(8,128)(2,1)S(1)}, u32[]{:S(2)}) copy-start(bf16[128,1088]{0,1:T(8,128)(2,1)S(1)} %add_convert_fusion) | copy-start | bytes 835588
  353.2 173.0 %all-gather.32.cloned.1.call-start = ((), (), s32[]{:S(2)}) async-start(), calls=%async_computation.20 | async-start | bytes 1392640 | tf_op jit(solution)/shard_map/all_gather | solution.py:418
  353.2 95.7 %slice-start = ((s8[9469952]{0:T(1024)(128)(4,1)}), s8[1081344]{0:T(1024)(128)(4,1)S(1)}, s32[]{:S(2)}) async-start(s8[9469952]{0:T(1024)(128)(4,1)} %bitcast.194), calls=%async_computation.28 | async-start | bytes 2162688
  353.8 208.8 %all-gather.34.cloned.1.call-start = ((), (), s32[]{:S(2)}) async-start(), calls=%async_computation.21 | async-start | bytes 1392640 | tf_op jit(solution)/shard_map/all_gather | solution.py:419
  354.5 248.3 %reduce-scatter.17.cloned.1.call-start = ((), (), s32[]{:S(2)}) async-start(), calls=%async_computation.18 | async-start | bytes 2949120 | tf_op jit(solution)/shard_map/reduce_scatter | solution.py:452
  441.2 7.7 slice-start.1
  441.2 7.7 slice-start.2
  448.9 2.8 copy-start.10
  448.9 2.8 copy-start.39
  455.7 2.3 copy-start.31
  455.9 2.4 copy-start.45
  457.8 2.5 copy-start.14
  460.3 4.6 copy-start.21
  464.9 2.4 copy-start.25
  469.5 2.9 copy-start.6
  488.7 154.5 %reduce-scatter.15.cloned.1.call-start = ((), (), s32[]{:S(2)}) async-start(), calls=%async_computation.17 | async-start | bytes 2949120 | tf_op jit(solution)/shard_map/reduce_scatter | solution.py:451
  498.8 178.9 %all-gather.30.cloned.1.call-start = ((), (), s32[]{:S(2)}) async-start(), calls=%async_computation.19 | async-start | bytes 1392640 | tf_op jit(solution)/shard_map/all_gather | solution.py:417
  499.4 255.8 %reduce-scatter.19.cloned.1.call-start = ((), (), s32[]{:S(2)}) async-start(), calls=%async_computation.24 | async-start | bytes 7520256
  520.1 8.9 all-to-all-start.1
  523.6 8.6 copy-start.11
  523.6 267.5 %reduce-scatter.23.cloned.1.call-start = ((), (), s32[]{:S(2)}) async-start(), calls=%async_computation.26 | async-start | bytes 1880064
  532.2 317.9 %reduce-scatter.25.cloned.1.call-start = ((), (), s32[]{:S(2)}) async-start(), calls=%async_computation.27 | async-start | bytes 5640192
  569.6 2.6 copy-start.15
  569.6 2.6 copy-start.17
  644.8 37.4 %copy-start.12 = (bf16[128,3264]{1,0:T(8,128)(2,1)}, bf16[128,3264]{1,0:T(8,128)(2,1)S(1)}, u32[]{:S(2)}) copy-start(bf16[128,3264]{1,0:T(8,128)(2,1)S(1)} %concatenate.20) | copy-start | bytes 2506756
  646.2 31.6 %all-to-all-start = ((bf16[128,4,816]{0,2,1:T(8,128)(2,1)}), bf16[128,4,816]{0,2,1:T(8,128)(2,1)S(1)}, u32[]{:S(2)}, u32[]{:S(2)}) async-start(bf16[128,4,816]{0,2,1:T(8,128)(2,1)} %bitcast.57), calls=%async_computation.2 | async-start | bytes 1671168 | tf_op jit(solution)/shard_map/all_to_all | solution.py:470
  649.7 249.1 %reduce-scatter.21.cloned.1.call-start = ((), (), s32[]{:S(2)}) async-start(), calls=%async_computation.25 | async-start | bytes 4386816
  682.3 10.5 %slice-start.3 = ((s8[7241728]{0:T(1024)(128)(4,1)}), s8[3047424]{0:T(1024)(128)(4,1)S(1)}, s32[]{:S(2)}) async-start(s8[7241728]{0:T(1024)(128)(4,1)} %bitcast.196), calls=%async_computation.31 | async-start | bytes 6094848
  684.0 8.8 slice-start.4
  684.0 8.8 copy-start.1
  684.0 8.8 copy-start.13
  (19 other events, 29.8 us)
Sparse Core Ops, SparseCore 0:
  25.0 73.6 all-gather.15
  100.6 28.6 all-gather.37
  131.1 29.3 all-gather.25
  162.8 26.8 all-gather.19
  191.9 26.8 all-gather.17
  221.0 32.6 all-gather.21
  255.3 90.1 all-gather.23
  347.2 93.9 all-gather.27
  443.0 53.1 all-gather.35
  497.9 28.2 all-gather.31
  528.0 34.4 all-gather.33
  565.4 37.3 reduce-scatter.16
  605.9 37.3 reduce-scatter.14
  644.9 32.7 all-gather.29
  679.9 75.2 reduce-scatter.18
  758.0 33.0 reduce-scatter.22
  793.8 56.2 reduce-scatter.24
  852.8 45.8 reduce-scatter.20
where the time goes:
time: 916 us; the launch traced here: 906 us
  waiting for transfers between devices  569 us (62%)
  blocking collectives  138 us (15%)
  matrix products  75.8 us (8%)
  local copies, waits for them, and re-layouts  66.5 us (7%)
  other arithmetic  29.2 us (3%)
  between operations  18.6 us (2%)
    unnamed x22, waiting for transfers between devices  153 us
    all_gather x1, waiting for transfers between devices, body(): lax.all_gather(matrix_cols[2], 'dp', axis=0, tiled=True)  88.4 us
    all_gather x1, waiting for transfers between devices, body(): lax.all_gather(matrix_cols[3], 'dp', axis=0, tiled=True)  86.2 us
    unnamed x2, blocking collectives  63.4 us
    reduce_scatter x1, waiting for transfers between devices, body(): lax.psum_scatter(grad_keys_all, 'ctx', scatter_dimension=0, tiled=True)  38.3 us
    all_gather x1, waiting for transfers between devices, body(): lax.all_gather(matrix_cols[0], 'dp', axis=0, tiled=True)  36.5 us
    reduce_scatter x1, waiting for transfers between devices, body(): lax.psum_scatter(grad_values_all, 'ctx', scatter_dimension=0, tiled=True)  29.9 us
    all_gather x1, waiting for transfers between devices, body(): lax.all_gather(attend_in, 'ctx', axis=0, tiled=True)  28 us
  transfers between devices with their start and end apart: 20, of which 18 were waited for; matrix products, arithmetic and copies ran while one was open for 18% of the time, Pallas kernels for 0%

commit v1 on v0

v1 whole, which is shorter than its diff:
```python
import numpy as np

import jax
import jax.numpy as jnp
from jax import lax
from jax.experimental import pallas as pl
from jax.experimental.pallas import tpu as pltpu
from jax.sharding import PartitionSpec as P

HEADS = 17
HEAD_DIM = 64

EPSILON = 1e-05
GELU_ROOT = 0.7978845608028654
GELU_CUBIC = 0.044715
MASKED = -1e30

BF = jnp.bfloat16
F32 = jnp.float32


def layer_norm(matrix, norm_gain, norm_shift):
    average = jnp.mean(matrix, axis=-1, keepdims=True)
    centered = matrix - average
    variance = jnp.mean(centered * centered, axis=-1, keepdims=True)
    inverse = lax.rsqrt(variance + EPSILON)
    normed = centered * inverse
    return (normed * norm_gain + norm_shift, normed, inverse)


def norm_backward(upstream, normed, inverse, norm_gain):
    grad_gain = jnp.sum(upstream * normed, axis=0)
    grad_shift = jnp.sum(upstream, axis=0)
    scaled = upstream * norm_gain
    centred_grad = (
        scaled
        - jnp.mean(scaled, axis=-1, keepdims=True)
        - normed * jnp.mean(scaled * normed, axis=-1, keepdims=True)
    )
    return (inverse * centred_grad, grad_gain, grad_shift)


def gelu_pair(before):
    cubic = GELU_ROOT * (before + GELU_CUBIC * before * before * before)
    tangent = jnp.tanh(cubic)
    result = 0.5 * before * (1.0 + tangent)
    derivative = 0.5 * (1.0 + tangent) + 0.5 * before * (1.0 - tangent * tangent) * GELU_ROOT * (
        1.0 + 3.0 * GELU_CUBIC * before * before
    )
    return (result, derivative)


def mm(left, right):
    return jnp.dot(left, right, preferred_element_type=F32)


def mm_nt(left, right):
    return lax.dot_general(left, right, (((1,), (1,)), ((), ())), preferred_element_type=F32)


def mm_tn(left, right):
    return lax.dot_general(left, right, (((0,), (0,)), ((), ())), preferred_element_type=F32)


def shuffle(blocks, me):
    blocks = list(blocks)
    step = 1
    while step < len(blocks):
        odd = (me // step) % 2 == 1
        blocks = [
            jnp.where(odd, blocks[at ^ step], blocks[at]) for at in range(len(blocks))
        ]
        step *= 2
    return blocks


def swap_with(value, axis, step):
    count = lax.axis_size(axis)
    return lax.ppermute(value, axis, [(at, at ^ step) for at in range(count)])


def exchange(blocks, axis):
    return [blocks[0]] + [
        swap_with(blocks[step], axis, step) for step in range(1, len(blocks))
    ]


def gather_rel(value, axis):
    return exchange([value] * lax.axis_size(axis), axis)


def reduce_rows(partial, axis):
    count = lax.axis_size(axis)
    rows = partial.shape[0] // count
    total = partial[:rows]
    for step in range(1, count):
        piece = partial[step * rows : (step + 1) * rows].astype(BF)
        total = total + swap_with(piece, axis, step).astype(F32)
    return total


def dp_reduce(grad, cores=2):
    count = lax.axis_size("dp")
    levels = count // cores
    index = lax.axis_index("dp")
    rows = grad.shape[0] // count
    width = grad.shape[1]
    view = grad.reshape(levels, cores, rows, width)
    core = index % cores
    keep = jnp.where(core == 0, view[:, 0], view[:, 1])
    away = jnp.where(core == 0, view[:, 1], view[:, 0]).astype(BF)
    keep = keep + swap_with(away, "dp", 1).astype(F32)
    blocks = shuffle([keep[at] for at in range(levels)], index // cores)
    total = blocks[0]
    for step in range(1, levels):
        total = total + swap_with(blocks[step].astype(BF), "dp", step * cores).astype(F32)
    return total


def head_tables(count, width, own_heads):
    share = own_heads * HEAD_DIM
    columns = 3 * width // count
    lists = {}
    most = 1
    for target in range(count):
        for place in range(3 * share):
            part, inner = divmod(place, share)
            column = target * share + inner
            if column < width:
                source, local = divmod(part * width + column, columns)
                lists.setdefault((source, target), []).append((local, place))
    most = max(len(entries) for entries in lists.values())
    send = np.full((count, count, most), -1, np.int32)
    put = np.full((count, count, most), -1, np.int32)
    for (source, target), entries in lists.items():
        for at, (local, place) in enumerate(entries):
            send[source, source ^ target, at] = local
            put[target, source ^ target, at] = place
    return send.reshape(count, -1), put.reshape(count, -1), most


def scores_of(query, key, row_pos, col_pos):
    score = mm_nt(query, key) * (HEAD_DIM ** (-0.5))
    return jnp.where(col_pos <= row_pos, score, MASKED)


def attend_kernel(own_heads, chunk, qkv_ref, row_ref, col_ref, mixed_ref, log_ref):
    rows = qkv_ref.shape[0]
    share = own_heads * HEAD_DIM
    col_pos = col_ref[...]
    for head in range(own_heads):
        span = slice(head * HEAD_DIM, (head + 1) * HEAD_DIM)
        key = qkv_ref[:, share + head * HEAD_DIM : share + (head + 1) * HEAD_DIM]
        value = qkv_ref[:, 2 * share + head * HEAD_DIM : 2 * share + (head + 1) * HEAD_DIM]
        for first in range(0, rows, chunk):
            part = slice(first, first + chunk)
            score = scores_of(qkv_ref[part, span], key, row_ref[part, :], col_pos)
            top = jnp.max(score, axis=-1, keepdims=True)
            log = top + jnp.log(jnp.sum(jnp.exp(score - top), axis=-1, keepdims=True))
            probs = jnp.exp(score - log).astype(BF)
            mixed_ref[part, span] = mm(probs, value).astype(BF)
            log_ref[part, head : head + 1] = log


def attend_back_kernel(
    own_heads, chunk, qkv_ref, row_ref, col_ref, log_ref, mixed_ref, grad_ref, out_ref, bias_ref
):
    rows = qkv_ref.shape[0]
    share = own_heads * HEAD_DIM
    scale = HEAD_DIM ** (-0.5)
    col_pos = col_ref[...]
    for head in range(own_heads):
        span = slice(head * HEAD_DIM, (head + 1) * HEAD_DIM)
        key_span = slice(share + head * HEAD_DIM, share + (head + 1) * HEAD_DIM)
        value_span = slice(2 * share + head * HEAD_DIM, 2 * share + (head + 1) * HEAD_DIM)
        key = qkv_ref[:, key_span]
        value = qkv_ref[:, value_span]
        grad_key = grad_value = grad_query_sum = None
        for first in range(0, rows, chunk):
            part = slice(first, first + chunk)
            query = qkv_ref[part, span]
            score = scores_of(query, key, row_ref[part, :], col_pos)
            exact = jnp.exp(score - log_ref[part, head : head + 1])
            grad = grad_ref[part, span]
            delta = jnp.sum(
                grad.astype(F32) * mixed_ref[part, span].astype(F32), axis=-1, keepdims=True
            )
            new_value = mm_tn(exact.astype(BF), grad)
            grad_score = (exact * (mm_nt(grad, value) - delta) * scale).astype(BF)
            grad_query = mm(grad_score, key)
            new_key = mm_tn(grad_score, query)
            new_sum = jnp.sum(grad_query, axis=0, keepdims=True)
            out_ref[part, span] = grad_query.astype(BF)
            if first == 0:
                grad_key, grad_value, grad_query_sum = new_key, new_value, new_sum
            else:
                grad_key = grad_key + new_key
                grad_value = grad_value + new_value
                grad_query_sum = grad_query_sum + new_sum
        out_ref[:, key_span] = grad_key.astype(BF)
        out_ref[:, value_span] = grad_value.astype(BF)
        bias_ref[0:1, span] = grad_query_sum
        bias_ref[1:2, span] = jnp.sum(grad_value, axis=0, keepdims=True)


def attend_forward(qkv, row_pos, col_pos, own_heads, chunk):
    rows = qkv.shape[0]
    return pl.pallas_call(
        lambda *refs: attend_kernel(own_heads, chunk, *refs),
        out_shape=(
            jax.ShapeDtypeStruct((rows, own_heads * HEAD_DIM), BF),
            jax.ShapeDtypeStruct((rows, own_heads), F32),
        ),
        name="attend",
    )(qkv, row_pos, col_pos)


def attend_backward(qkv, row_pos, col_pos, log, mixed, grad, own_heads, chunk):
    rows = qkv.shape[0]
    return pl.pallas_call(
        lambda *refs: attend_back_kernel(own_heads, chunk, *refs),
        out_shape=(
            jax.ShapeDtypeStruct((rows, 3 * own_heads * HEAD_DIM), BF),
            jax.ShapeDtypeStruct((2, own_heads * HEAD_DIM), F32),
        ),
        name="attend_back",
    )(qkv, row_pos, col_pos, log, mixed, grad)


def body(
    block_input,
    block_pairs,
    attend_gain,
    attend_shift,
    input_weight,
    query_bias,
    value_bias,
    output_weight,
    output_bias,
    feed_gain,
    feed_shift,
    expand_weight,
    expand_bias,
    reduce_weight,
    reduce_bias,
    output_cotangent,
):
    inputs = block_input[0]
    cotangent = output_cotangent[0]
    rows, width = inputs.shape
    count = lax.axis_size("ctx")
    groups = lax.axis_size("dp")
    me = lax.axis_index("ctx")
    half = rows // 2
    own_heads = -(-HEADS // count)
    share = own_heads * HEAD_DIM
    padded = share * count
    shard_rows = input_weight.shape[0]
    shard_columns = output_weight.shape[1]
    hidden = reduce_weight.shape[0] * groups
    unit = hidden // (groups * count)
    hidden_share = hidden // count
    spans = groups // count
    chunk = min(rows * count, (1 << 18) // (rows * count))

    own_expand_bias = lax.dynamic_slice_in_dim(expand_bias, me * unit, unit)
    small = jnp.stack(
        [
            attend_gain,
            attend_shift,
            query_bias,
            value_bias,
            output_bias,
            feed_gain,
            feed_shift,
            reduce_bias,
        ]
    )
    both = jnp.concatenate([small.reshape(-1), own_expand_bias])
    gathered = shuffle(gather_rel(both, "dp"), lax.axis_index("dp"))
    cut = 8 * shard_rows
    vectors = jnp.stack([piece[:cut].reshape(8, shard_rows) for piece in gathered], axis=1)
    vectors = vectors.reshape(8, width).astype(F32)
    own_expand = jnp.concatenate([piece[cut:] for piece in gathered]).astype(F32)
    pad = padded - width
    own_query_bias = lax.dynamic_slice_in_dim(jnp.pad(vectors[2], (0, pad)), me * share, share)
    own_value_bias = lax.dynamic_slice_in_dim(jnp.pad(vectors[3], (0, pad)), me * share, share)
    proj_bias = jnp.concatenate([own_query_bias, jnp.zeros((share,), F32), own_value_bias])

    send_table, put_table, most = head_tables(count, width, own_heads)
    send_at = lax.dynamic_index_in_dim(jnp.asarray(send_table), me, keepdims=False)
    put_at = lax.dynamic_index_in_dim(jnp.asarray(put_table), me, keepdims=False)
    pick = (lax.broadcasted_iota(jnp.int32, (input_weight.shape[1], count * most), 0)
            == send_at[None, :]).astype(BF)
    place = (lax.broadcasted_iota(jnp.int32, (count * most, 3 * share), 1)
             == put_at[:, None]).astype(BF)
    picked = mm(input_weight, pick).astype(BF)
    arrived = exchange(
        [picked[:, step * most : (step + 1) * most] for step in range(count)], "ctx"
    )
    own_input = mm(jnp.concatenate(arrived, axis=1), place).astype(BF)
    full_input = lax.all_gather(own_input, "dp", axis=0, tiled=True)

    output_parts = shuffle(gather_rel(output_weight, "ctx"), me)
    full_output = lax.all_gather(
        jnp.concatenate(output_parts, axis=1), "dp", axis=0, tiled=True
    )
    expand_view = expand_weight.reshape(shard_rows, spans, count, unit)
    expand_parts = shuffle(
        exchange(
            shuffle(
                [
                    expand_view[:, :, at].reshape(shard_rows, spans * unit)
                    for at in range(count)
                ],
                me,
            ),
            "ctx",
        ),
        me,
    )
    full_expand = lax.all_gather(
        jnp.concatenate(expand_parts, axis=1), "dp", axis=0, tiled=True
    )
    reduce_view = reduce_weight.reshape(count, unit, shard_columns)
    reduce_parts = shuffle(
        exchange(shuffle([reduce_view[at] for at in range(count)], me), "ctx"), me
    )
    full_reduce = lax.all_gather(
        jnp.concatenate(reduce_parts, axis=1), "dp", axis=0, tiled=True
    )

    pair_list = shuffle([block_pairs[at] for at in range(count)], me)
    inner = jnp.arange(half, dtype=jnp.int32)
    positions = jnp.concatenate(
        [
            piece
            for pair in pair_list
            for piece in (pair * half + inner, (2 * count - 1 - pair) * half + inner)
        ]
    )
    row_pos = positions[:, None]
    col_pos = positions[None, :]

    normed_in, first_normed, first_inverse = layer_norm(inputs, vectors[0], vectors[1])
    attend_in = normed_in.astype(BF)
    attend_all = jnp.concatenate(gather_rel(attend_in, "ctx"))
    cot_low = cotangent.astype(BF)
    cot_all = jnp.concatenate(gather_rel(cot_low, "ctx"))
    qkv = (mm(attend_all, full_input) + proj_bias).astype(BF)
    own_mixed, log = attend_forward(qkv, row_pos, col_pos, own_heads, chunk)
    mixed_parts = shuffle(
        exchange([own_mixed[at * rows : (at + 1) * rows] for at in range(count)], "ctx"), me
    )
    mixed = jnp.concatenate(mixed_parts, axis=1)[:, :width]
    resid = inputs + mm(mixed, full_output) + vectors[4]
    normed_mid, second_normed, second_inverse = layer_norm(resid, vectors[5], vectors[6])
    feed_in = normed_mid.astype(BF)
    feed_all = jnp.concatenate(gather_rel(feed_in, "ctx"))
    before = mm(feed_all, full_expand) + own_expand
    activated, slope = gelu_pair(before)
    activ_low = activated.astype(BF)

    grad_before = mm_nt(cot_all, full_reduce) * slope
    before_low = grad_before.astype(BF)
    grad_expand_bias = jnp.sum(grad_before, axis=0)
    grad_feed_in = reduce_rows(mm_nt(before_low, full_expand), "ctx")
    output = resid + reduce_rows(mm(activ_low, full_reduce), "ctx") + vectors[7]
    grad_mid, grad_feed_gain, grad_feed_shift = norm_backward(
        grad_feed_in, second_normed, second_inverse, vectors[5]
    )
    grad_resid = cotangent + grad_mid
    resid_low = grad_resid.astype(BF)
    grad_mixed = jnp.pad(mm_nt(resid_low, full_output).astype(BF), ((0, 0), (0, pad)))
    own_grad_mixed = jnp.concatenate(
        exchange(
            shuffle([grad_mixed[:, at * share : (at + 1) * share] for at in range(count)], me),
            "ctx",
        )
    )
    grad_reduce = dp_reduce(mm_tn(activ_low, cot_all))
    grad_expand = dp_reduce(mm_tn(feed_all, before_low))
    mixed_all = jnp.concatenate(gather_rel(mixed, "ctx"))
    resid_cols = jnp.concatenate(
        exchange(
            shuffle(
                [
                    resid_low[:, at * shard_columns : (at + 1) * shard_columns]
                    for at in range(count)
                ],
                me,
            ),
            "ctx",
        )
    )
    grad_output_weight = dp_reduce(mm_tn(mixed_all, resid_cols))

    grad_proj, proj_sums = attend_backward(
        qkv, row_pos, col_pos, log, own_mixed, own_grad_mixed, own_heads, chunk
    )
    grad_attend_in = reduce_rows(mm_nt(grad_proj, full_input), "ctx")
    grad_first, grad_attend_gain, grad_attend_shift = norm_backward(
        grad_attend_in, first_normed, first_inverse, vectors[0]
    )
    input_grad = grad_resid + grad_first
    grad_input = dp_reduce(mm_tn(attend_all, grad_proj)).astype(BF)

    back_input = mm_nt(grad_input, place).astype(BF)
    back_input = exchange(
        [back_input[:, step * most : (step + 1) * most] for step in range(count)], "ctx"
    )
    grad_input_weight = mm_nt(jnp.concatenate(back_input, axis=1), pick)
    back_reduce = grad_reduce.astype(BF)
    back_reduce = shuffle(
        exchange(
            shuffle(
                [
                    back_reduce[:, at * shard_columns : (at + 1) * shard_columns]
                    for at in range(count)
                ],
                me,
            ),
            "ctx",
        ),
        me,
    )
    grad_reduce_weight = jnp.concatenate(back_reduce, axis=0).astype(F32)
    back_expand = grad_expand.astype(BF)
    back_expand = shuffle(
        exchange(
            shuffle(
                [
                    back_expand[:, at * spans * unit : (at + 1) * spans * unit]
                    for at in range(count)
                ],
                me,
            ),
            "ctx",
        ),
        me,
    )
    grad_expand_weight = jnp.stack(
        [piece.reshape(shard_rows, spans, unit) for piece in back_expand], axis=2
    ).reshape(shard_rows, spans * count * unit).astype(F32)

    def widen(piece):
        whole = lax.dynamic_update_slice(jnp.zeros((padded,), F32), piece, (me * share,))
        return whole[:width]

    stacked = jnp.stack(
        [
            grad_attend_gain,
            grad_attend_shift,
            widen(proj_sums[0]),
            widen(proj_sums[1]),
            jnp.sum(grad_resid, axis=0),
            grad_feed_gain,
            grad_feed_shift,
            jnp.sum(cotangent, axis=0),
        ]
    )
    slots = (jnp.arange(count) == me).astype(F32)
    hidden_sums = grad_expand_bias.reshape(groups, 1, unit) * slots[None, :, None]
    vector_rows = stacked.reshape(8, groups, shard_rows).transpose(1, 0, 2).reshape(groups, -1)
    all_rows = jnp.concatenate([vector_rows, hidden_sums.reshape(groups, -1)], axis=1)
    dp_blocks = exchange(
        shuffle([all_rows[at] for at in range(groups)], lax.axis_index("dp")), "dp"
    )
    dp_total = sum(dp_blocks[1:], dp_blocks[0])
    ctx_blocks = gather_rel(dp_total, "ctx")
    total = sum(ctx_blocks[1:], ctx_blocks[0])
    sums = total[:cut].reshape(8, shard_rows)
    return (
        output[None],
        input_grad[None],
        sums[0],
        sums[1],
        grad_input_weight,
        sums[2],
        sums[3],
        grad_output_weight,
        sums[4],
        sums[5],
        sums[6],
        grad_expand_weight,
        total[cut:],
        grad_reduce_weight,
        sums[7],
    )


def solution(mesh):
    matrix = P("dp", "ctx")
    vector = P("dp")
    tokens = P("dp", "ctx", None)
    return jax.shard_map(
        body,
        mesh=mesh,
        in_specs=(
            tokens,
            P(),
            vector,
            vector,
            matrix,
            vector,
            vector,
            matrix,
            vector,
            vector,
            vector,
            matrix,
            vector,
            matrix,
            vector,
            tokens,
        ),
        out_specs=(
            tokens,
            tokens,
            vector,
            vector,
            matrix,
            vector,
            vector,
            matrix,
            vector,
            vector,
            vector,
            matrix,
            vector,
            matrix,
            vector,
        ),
        check_vma=False,
    )
```

time: 916 us -> 393 us (0.43)
  waiting for transfers between devices: 569 us -> 133 us
  blocking collectives: 138 us -> 0 us
  starting transfers between devices: 8.31 us -> 107 us
  local copies, waits for them, and re-layouts: 66.5 us -> 32.4 us
  matrix products: 75.8 us -> 47.8 us
  Pallas kernels: 0 us -> 17.6 us
    all_gather x12 -> x4, waiting for transfers between devices: 346 us -> 15.1 us  [the longest x1 15.1 us: body(): lax.all_gather(jnp.concatenate(reduce_parts, axis=1), 'dp', axis=0, tiled...]
    unnamed x22 -> x4, waiting for transfers between devices: 153 us -> 0.07 us
    ppermute x0 -> x84, waiting for transfers between devices: none -> 118 us  [swap_with(): return lax.ppermute(value, axis, [(at, at ^ step) for at in range(count)])]
    ppermute x0 -> x84, starting transfers between devices: none -> 106 us  [swap_with(): return lax.ppermute(value, axis, [(at, at ^ step) for at in range(count)])]
    reduce_scatter x2 -> x0, waiting for transfers between devices: 68.2 us -> none  [the longest x1 38.3 us: body(): lax.psum_scatter(grad_keys_all, 'ctx', scatter_dimension=0, tiled=True)]
    unnamed x2 -> x0, blocking collectives: 63.4 us -> none
    all_to_all x2 -> x0, blocking collectives: 32.5 us -> none  [the longest x1 20.1 us: body(): lax.all_to_all(before_low, 'ctx', split_axis=1, concat_axis=0, tiled=True)]
    all_gather x2 -> x0, blocking collectives: 26.5 us -> none  [the longest x1 15.4 us: body(): lax.all_gather(input_weight, 'ctx', axis=1, tiled=True)]
  transfers between devices with their start and end apart: 20 -> 88, of which waited for: 18 -> 38; matrix products, arithmetic and copies ran while one was open for 18% -> 24% of each run, Pallas kernels for 0% -> 5%
where the time goes in v1:
time: 393 us; the launch traced here: 387 us
  waiting for transfers between devices  133 us (34%)
  starting transfers between devices  107 us (27%)
  matrix products  47.8 us (12%)
  local copies, waits for them, and re-layouts  32.4 us (8%)
  other arithmetic  28.9 us (7%)
  between operations  20.9 us (5%)
  Pallas kernels  17.6 us (4%)
    ppermute x84, waiting for transfers between devices, swap_with(): return lax.ppermute(value, axis, [(at, at ^ step) for at in range(count)])  118 us
    ppermute x84, starting transfers between devices, swap_with(): return lax.ppermute(value, axis, [(at, at ^ step) for at in range(count)])  106 us
    dot_general x6, matrix products, mm(): return jnp.dot(left, right, preferred_element_type=F32)  18.5 us
    dot_general x6, matrix products, mm_nt(): lax.dot_general(left, right, (((1,), (1,)), ((), ())), preferred_element_...  18.5 us
    all_gather x1, waiting for transfers between devices, body(): lax.all_gather(jnp.concatenate(reduce_parts, axis=1), 'dp', axis=0, tiled...  15.1 us
    dot_general x4, matrix products, mm_tn(): lax.dot_general(left, right, (((0,), (0,)), ((), ())), preferred_element_...  10.8 us
    pallas_call x1, Pallas kernels, attend_forward(): pl.pallas_call(lambda *refs: attend_kernel(own_heads, chunk, *refs), out_...  9.48 us
    pallas_call x1, Pallas kernels, attend_backward(): pl.pallas_call(lambda *refs: attend_back_kernel(own_heads, chunk, *refs),...  8.13 us
  transfers between devices with their start and end apart: 88, of which 38 were waited for; matrix products, arithmetic and copies ran while one was open for 24% of the time, Pallas kernels for 5%

profile of v1, /device:TPU:0, one launch (start us, length us, event | category | flops | bytes accessed | tf_op | source)
XLA Modules:
  0.0 387.4 jit_solution(8012426737211078950)
XLA Ops:
  9.3 3.0 collective-permute-start.10
  15.5 2.6 collective-permute-done.11
  19.6 2.0 fusion.19
  26.5 2.0 collective-permute-done.16
  37.5 2.2 collective-permute-done.22
  43.1 1.6 collective-permute-start.5
  44.9 2.5 collective-permute-start.3
  54.5 3.6 collective-permute-start.1
  68.7 1.5 collective-permute-start.9
  73.5 5.7 %collective-permute-done.9 = bf16[128,1088]{0,1:T(8,128)(2,1)S(1)} collective-permute-done((bf16[128,1088]{0,1:T(8,128)(2,1)S(1)}, bf16[128,1088]{0,1:T(8,128)(2,1)S(1)}, u32[]{:S(2)}, u32[]{:S(2)}) %collective-permute-start.9) | collective-permute-done | bytes 278560 | tf_op jit(solution)/shard_map/ppermute | solution.py:79
  79.2 4.2 %collective-permute-done.8 = bf16[128,1088]{0,1:T(8,128)(2,1)S(1)} collective-permute-done((bf16[128,1088]{0,1:T(8,128)(2,1)S(1)}, bf16[128,1088]{0,1:T(8,128)(2,1)S(1)}, u32[]{:S(2)}, u32[]{:S(2)}) %collective-permute-start.8) | collective-permute-done | bytes 278560 | tf_op jit(solution)/shard_map/ppermute | solution.py:79
  83.5 4.4 %add_convert_fusion.refs_0_ = bf16[512,960]{1,0:T(8,128)(2,1)} fusion(bf16[1088,960]{1,0:T(8,128)(2,1)} %all-gather.5.cloned.1.call-done, f32[960]{0:T(1024)S(1)} %pad_maximum_fusion.12, bf16[128,1088]{0,1:T(8,128)(2,1)S(1)} %collective-permute-done.9, bf16[128,1088]{0,1:T(8,128)(2,1)S(1)} %collective-permute-done.8, ...), kind=kOutput, calls=%fused_computation.34 | convolution fusion | flops 1074987008 | bytes 4189952 | tf_op jit(solution)/shard_map/dot_general | solution.py:54
  87.9 9.5 %attend.1 = (bf16[512,320]{1,0:T(8,128)(2,1)}, f32[512,5]{1,0:T(8,128)}) custom-call(bf16[512,960]{1,0:T(8,128)(2,1)} %add_convert_fusion.refs_0_, s32[512,1]{1,0:T(8,128)} %copy.136.refs_1_, s32[1,512]{1,0:T(1,128)} %bitcast.217), custom_call_target="tpu_custom_call" | custom-call | tf_op jit(solution)/shard_map/attend/pallas_call | solution.py:208
  102.2 2.6 collective-permute-done.14
  107.8 2.9 fusion.125
  111.3 1.6 collective-permute-start.21
  115.2 1.6 collective-permute-start.33
  118.8 3.1 collective-permute-done.21
  122.9 5.0 %collective-permute-done.20 = bf16[128,1088]{0,1:T(8,128)(2,1)} collective-permute-done((bf16[128,1088]{0,1:T(8,128)(2,1)S(1)}, bf16[128,1088]{0,1:T(8,128)(2,1)}, u32[]{:S(2)}, u32[]{:S(2)}) %collective-permute-start.20) | collective-permute-done | bytes 278560 | tf_op jit(solution)/shard_map/ppermute | solution.py:79
  130.4 5.1 %convolution_add_fusion = f32[512,1088]{0,1:T(8,128)} fusion(bf16[1088,1088]{1,0:T(8,128)(2,1)} %all-gather.9.cloned.1.call-done, f32[1088]{0:T(1024)S(1)} %convert_element_type.266, bf16[128,1088]{0,1:T(8,128)(2,1)} %collective-permute-done.21, bf16[128,1088]{0,1:T(8,128)(2,1)} %collective-permute-done.20, bf16[128,1088]{0,1:T(8,128)(2,1)} %collective-permute-done.19, ...), kind=kOutput, calls=%fused_computation.7 | convolution fusion | flops 1217167360 | bytes 5714176 | tf_op jit(solution)/shard_map/dot_general | solution.py:54
  135.5 4.4 %collective-permute-done.32 = bf16[128,1088]{0,1:T(8,128)(2,1)} collective-permute-done((bf16[128,1088]{0,1:T(8,128)(2,1)S(1)}, bf16[128,1088]{0,1:T(8,128)(2,1)}, u32[]{:S(2)}, u32[]{:S(2)}) %collective-permute-start.32) | collective-permute-done | bytes 278560 | tf_op jit(solution)/shard_map/ppermute | solution.py:79
  139.9 15.1 %all-gather.11.cloned.1.call-done = bf16[1088,1088]{1,0:T(8,128)(2,1)} async-done(((bf16[136,1088]{1,0:T(8,128)(2,1)}), bf16[1088,1088]{1,0:T(8,128)(2,1)}) %all-gather.11.cloned.1.call-update) | async-done | bytes 2367504 | tf_op jit(solution)/shard_map/all_gather | solution.py:329
  155.0 5.5 %fusion.129 = (f32[1088]{0:T(1024)S(1)}, bf16[512,1088]{0,1:T(8,128)(2,1)S(1)}) fusion(f32[512,1088]{0,1:T(8,128)} %convolution_add_fusion, bf16[1088,1088]{1,0:T(8,128)(2,1)} %all-gather.11.cloned.1.call-done, bf16[128,1088]{0,1:T(8,128)(2,1)} %collective-permute-done.33, bf16[128,1088]{0,1:T(8,128)(2,1)} %collective-permute-done.32, ...), kind=kOutput, calls=%fused_computation.401 | convolution fusion | flops 1227750400 | bytes 6828288 | tf_op jit(solution)/shard_map/dot_general | solution.py:58
  160.5 3.0 fusion.126
  164.3 2.4 collective-permute-start.36
  167.8 2.8 fusion.49
  170.7 2.5 copy-done.4
  174.5 3.1 fusion.75
  178.9 2.2 copy-done.31
  181.2 3.1 fusion.127
  185.3 2.4 collective-permute-start.30
  188.9 2.1 multiply_reduce_fusion
  191.0 5.1 %collective-permute-done.30 = bf16[128,1088]{0,1:T(8,128)(2,1)S(1)} collective-permute-done((bf16[128,1088]{0,1:T(8,128)(2,1)}, bf16[128,1088]{0,1:T(8,128)(2,1)S(1)}, u32[]{:S(2)}, u32[]{:S(2)}) %collective-permute-start.30) | collective-permute-done | bytes 278560 | tf_op jit(solution)/shard_map/ppermute | solution.py:79
  197.6 2.9 collective-permute-done.29
  200.4 1.6 collective-permute-done.28
  202.1 2.4 fusion.111
  215.0 2.0 fusion.20
  220.4 8.1 %attend_back.1 = (bf16[512,960]{1,0:T(8,128)(2,1)}, f32[2,320]{1,0:T(2,128)}) custom-call(bf16[512,960]{1,0:T(8,128)(2,1)} %add_convert_fusion.refs_0_, s32[512,1]{1,0:T(8,128)} %copy.136.refs_1_, s32[1,512]{1,0:T(1,128)} %bitcast.218, f32[512,5]{1,0:T(8,128)} %get-tuple-element.20.refs_3_, bf16[512,320]{1,0:T(8,128)(2,1)} %get-tuple-element.19.refs_4_, ...), custom_call_target="tpu_custom_call" | custom-call | tf_op jit(solution)/shard_map/attend_back/pallas_call | solution.py:220
  228.6 4.7 %fusion.128 = (bf16[512,1088]{0,1:T(8,128)(2,1)S(1)}, f32[512,1088]{0,1:T(8,128)}) fusion(bf16[512,960]{1,0:T(8,128)(2,1)} %get-tuple-element.21, bf16[1088,960]{1,0:T(8,128)(2,1)} %all-gather.5.cloned.1.call-done), kind=kOutput, calls=%fused_computation.400 | convolution fusion | flops 1070104576 | bytes 6414336 | tf_op jit(solution)/shard_map/dot_general | solution.py:58
  238.0 2.9 fusion.76
  242.3 1.7 collective-permute-done.42
  244.0 5.0 %collective-permute-done.41 = bf16[128,1088]{0,1:T(8,128)(2,1)} collective-permute-done((bf16[128,1088]{0,1:T(8,128)(2,1)S(1)}, bf16[128,1088]{0,1:T(8,128)(2,1)}, u32[]{:S(2)}, u32[]{:S(2)}) %collective-permute-start.41) | collective-permute-done | bytes 278560 | tf_op jit(solution)/shard_map/ppermute | solution.py:79
  249.0 1.9 multiply_reduce_fusion.1
  253.0 2.3 collective-permute-start.48
  256.3 2.7 collective-permute-start.46
  259.0 1.6 collective-permute-start.44
  260.9 1.6 fusion.30
  267.5 1.6 collective-permute-start.69
  273.3 1.9 collective-permute-done.69
  275.2 3.6 collective-permute-done.68
  279.6 3.2 bitcast_add_fusion.1
  283.0 1.7 collective-permute-start.73
  284.7 2.8 collective-permute-start.71
  287.9 1.7 collective-permute-start.80
  291.3 4.0 %collective-permute-done.73 = bf16[136,1088]{1,0:T(8,128)(2,1)S(1)} collective-permute-done((bf16[136,1088]{1,0:T(8,128)(2,1)S(1)}, bf16[136,1088]{1,0:T(8,128)(2,1)S(1)}, u32[]{:S(2)}, u32[]{:S(2)}) %collective-permute-start.73) | collective-permute-done | bytes 295968 | tf_op jit(solution)/shard_map/ppermute | solution.py:79
  295.2 12.6 %collective-permute-start.78 = (bf16[136,1088]{1,0:T(8,128)(2,1)S(1)}, bf16[136,1088]{1,0:T(8,128)(2,1)S(1)}, u32[]{:S(2)}, u32[]{:S(2)}) collective-permute-start(bf16[136,1088]{1,0:T(8,128)(2,1)S(1)} %get-tuple-element.136), channel_id=1, source_target_pairs={{0,8},{4,12},{8,0},{12,4},{16,24},{20,28},{24,16},{28,20},{1,9},{5... | collective-permute-start | bytes 887816 | tf_op jit(solution)/shard_map/ppermute | solution.py:79
  307.8 18.0 %collective-permute-done.72 = bf16[136,1088]{1,0:T(8,128)(2,1)S(1)} collective-permute-done((bf16[136,1088]{1,0:T(8,128)(2,1)S(1)}, bf16[136,1088]{1,0:T(8,128)(2,1)S(1)}, u32[]{:S(2)}, u32[]{:S(2)}) %collective-permute-start.72) | collective-permute-done | bytes 295968 | tf_op jit(solution)/shard_map/ppermute | solution.py:79
  325.8 1.6 collective-permute-start.56
  329.4 21.8 %collective-permute-done.79 = bf16[136,1088]{1,0:T(8,128)(2,1)S(1)} collective-permute-done((bf16[136,1088]{1,0:T(8,128)(2,1)S(1)}, bf16[136,1088]{1,0:T(8,128)(2,1)S(1)}, u32[]{:S(2)}, u32[]{:S(2)}) %collective-permute-start.79) | collective-permute-done | bytes 295968 | tf_op jit(solution)/shard_map/ppermute | solution.py:79
  358.8 3.0 collective-permute-done.81
  364.3 3.0 reshape.456
  368.4 2.6 fusion.8
  372.9 1.8 collective-permute-start.59
  378.6 1.8 fusion.2
  (415 shorter events, 117.8 us)
Async XLA Ops:
  7.2 76.3 %all-gather.5.cloned.1.call-start = ((), (), s32[]{:S(2)}) async-start(), calls=%async_computation | async-start | bytes 2506752 | tf_op jit(solution)/shard_map/all_gather | solution.py:302
  9.3 6.2 %collective-permute-start.10 = (bf16[136,320]{1,0:T(8,128)(2,1)S(1)}, bf16[136,320]{1,0:T(8,128)(2,1)S(1)}, u32[]{:S(2)}, u32[]{:S(2)}) collective-permute-start(bf16[136,320]{1,0:T(8,128)(2,1)S(1)} %get-tuple-element.205), channel_id=1, source_target_pairs={{0,1},{1,0},{2,3},{3,2},{4,5},{5,4},{6,7},{7,6},{8,9},{9,8},{10,11... | collective-permute-start | bytes 261128 | tf_op jit(solution)/shard_map/ppermute | solution.py:79
  21.7 86.1 %all-gather.7.cloned.1.call-start = ((), (), s32[]{:S(2)}) async-start(), calls=%async_computation.1 | async-start | bytes 2820096 | tf_op jit(solution)/shard_map/all_gather | solution.py:305
  30.1 100.3 %all-gather.9.cloned.1.call-start = ((), (), s32[]{:S(2)}) async-start(), calls=%async_computation.2 | async-start | bytes 2820096 | tf_op jit(solution)/shard_map/all_gather | solution.py:322
  41.4 113.5 %all-gather.11.cloned.1.call-start = ((), (), s32[]{:S(2)}) async-start(), calls=%async_computation.3 | async-start | bytes 2820096 | tf_op jit(solution)/shard_map/all_gather | solution.py:329
  43.1 11.4 %collective-permute-start.6 = (bf16[1224]{0:T(1024)(128)(2,1)S(1)}, bf16[1224]{0:T(1024)(128)(2,1)S(1)}, u32[]{:S(2)}, u32[]{:S(2)}) collective-permute-start(bf16[1224]{0:T(1024)(128)(2,1)S(1)} %pad_maximum_fusion.11), channel_id=1, source_target_pairs={{0,4},{4,0},{8,12},{12,8},{16,20},{20,16},{24,28},{28,24},{1,5},{5... | collective-permute-start | bytes 7352 | tf_op jit(solution)/shard_map/ppermute | solution.py:79
  43.1 15.1 %collective-permute-start.5 = (bf16[1224]{0:T(1024)(128)(2,1)S(1)}, bf16[1224]{0:T(1024)(128)(2,1)S(1)}, u32[]{:S(2)}, u32[]{:S(2)}) collective-permute-start(bf16[1224]{0:T(1024)(128)(2,1)S(1)} %pad_maximum_fusion.11), channel_id=1, source_target_pairs={{0,8},{4,12},{8,0},{12,4},{16,24},{20,28},{24,16},{28,20},{1,9},{5... | collective-permute-start | bytes 7352 | tf_op jit(solution)/shard_map/ppermute | solution.py:79
  44.7 13.6 %collective-permute-start.4 = (bf16[1224]{0:T(1024)(128)(2,1)S(1)}, bf16[1224]{0:T(1024)(128)(2,1)S(1)}, u32[]{:S(2)}, u32[]{:S(2)}) collective-permute-start(bf16[1224]{0:T(1024)(128)(2,1)S(1)} %pad_maximum_fusion.11), channel_id=1, source_target_pairs={{0,12},{4,8},{8,4},{12,0},{16,28},{20,24},{24,20},{28,16},{1,13},{... | collective-permute-start | bytes 7352 | tf_op jit(solution)/shard_map/ppermute | solution.py:79
  44.9 14.3 %collective-permute-start.3 = (bf16[1224]{0:T(1024)(128)(2,1)S(1)}, bf16[1224]{0:T(1024)(128)(2,1)S(1)}, u32[]{:S(2)}, u32[]{:S(2)}) collective-permute-start(bf16[1224]{0:T(1024)(128)(2,1)S(1)} %pad_maximum_fusion.11), channel_id=1, source_target_pairs={{0,16},{4,20},{8,24},{12,28},{16,0},{20,4},{24,8},{28,12},{1,17},{... | collective-permute-start | bytes 7352 | tf_op jit(solution)/shard_map/ppermute | solution.py:79
  47.5 13.3 %collective-permute-start.2 = (bf16[1224]{0:T(1024)(128)(2,1)S(1)}, bf16[1224]{0:T(1024)(128)(2,1)S(1)}, u32[]{:S(2)}, u32[]{:S(2)}) collective-permute-start(bf16[1224]{0:T(1024)(128)(2,1)S(1)} %pad_maximum_fusion.11), channel_id=1, source_target_pairs={{0,20},{4,16},{8,28},{12,24},{16,4},{20,0},{24,12},{28,8},{1,21},{... | collective-permute-start | bytes 7352 | tf_op jit(solution)/shard_map/ppermute | solution.py:79
  54.5 7.3 %collective-permute-start.1 = (bf16[1224]{0:T(1024)(128)(2,1)S(1)}, bf16[1224]{0:T(1024)(128)(2,1)S(1)}, u32[]{:S(2)}, u32[]{:S(2)}) collective-permute-start(bf16[1224]{0:T(1024)(128)(2,1)S(1)} %pad_maximum_fusion.11), channel_id=1, source_target_pairs={{0,24},{4,28},{8,16},{12,20},{16,8},{20,12},{24,0},{28,4},{1,25},{... | collective-permute-start | bytes 7352 | tf_op jit(solution)/shard_map/ppermute | solution.py:79
  58.3 7.0 %collective-permute-start.26 = (bf16[136,272]{1,0:T(8,128)(2,1)S(1)}, bf16[136,272]{1,0:T(8,128)(2,1)S(1)}, u32[]{:S(2)}, u32[]{:S(2)}) collective-permute-start(bf16[136,272]{1,0:T(8,128)(2,1)S(1)} %get-tuple-element.187), channel_id=1, source_target_pairs={{0,2},{1,3},{2,0},{3,1},{4,6},{5,7},{6,4},{7,5},{8,10},{9,11},{10,... | collective-permute-start | bytes 221960 | tf_op jit(solution)/shard_map/ppermute | solution.py:79
  59.3 6.7 %collective-permute-start.25 = (bf16[136,272]{1,0:T(8,128)(2,1)S(1)}, bf16[136,272]{1,0:T(8,128)(2,1)S(1)}, u32[]{:S(2)}, u32[]{:S(2)}) collective-permute-start(bf16[136,272]{1,0:T(8,128)(2,1)S(1)} %get-tuple-element.186), channel_id=1, source_target_pairs={{0,3},{1,2},{2,1},{3,0},{4,7},{5,6},{6,5},{7,4},{8,11},{9,10},{10,... | collective-permute-start | bytes 221960 | tf_op jit(solution)/shard_map/ppermute | solution.py:79
  60.8 6.1 %collective-permute-start.27 = (bf16[136,272]{1,0:T(8,128)(2,1)S(1)}, bf16[136,272]{1,0:T(8,128)(2,1)S(1)}, u32[]{:S(2)}, u32[]{:S(2)}) collective-permute-start(bf16[136,272]{1,0:T(8,128)(2,1)S(1)} %get-tuple-element.185), channel_id=1, source_target_pairs={{0,1},{1,0},{2,3},{3,2},{4,5},{5,4},{6,7},{7,6},{8,9},{9,8},{10,11... | collective-permute-start | bytes 221960 | tf_op jit(solution)/shard_map/ppermute | solution.py:79
  68.7 10.5 %collective-permute-start.9 = (bf16[128,1088]{0,1:T(8,128)(2,1)S(1)}, bf16[128,1088]{0,1:T(8,128)(2,1)S(1)}, u32[]{:S(2)}, u32[]{:S(2)}) collective-permute-start(bf16[128,1088]{0,1:T(8,128)(2,1)S(1)} %add_convert_fusion.2), channel_id=1, source_target_pairs={{0,3},{1,2},{2,1},{3,0},{4,7},{5,6},{6,5},{7,4},{8,11},{9,10},{10,... | collective-permute-start | bytes 835592 | tf_op jit(solution)/shard_map/ppermute | solution.py:79
  70.2 13.2 %collective-permute-start.8 = (bf16[128,1088]{0,1:T(8,128)(2,1)S(1)}, bf16[128,1088]{0,1:T(8,128)(2,1)S(1)}, u32[]{:S(2)}, u32[]{:S(2)}) collective-permute-start(bf16[128,1088]{0,1:T(8,128)(2,1)S(1)} %add_convert_fusion.2), channel_id=1, source_target_pairs={{0,2},{1,3},{2,0},{3,1},{4,6},{5,7},{6,4},{7,5},{8,10},{9,11},{10,... | collective-permute-start | bytes 835592 | tf_op jit(solution)/shard_map/ppermute | solution.py:79
  71.2 12.2 %collective-permute-start.7 = (bf16[128,1088]{0,1:T(8,128)(2,1)S(1)}, bf16[128,1088]{0,1:T(8,128)(2,1)S(1)}, u32[]{:S(2)}, u32[]{:S(2)}) collective-permute-start(bf16[128,1088]{0,1:T(8,128)(2,1)S(1)} %add_convert_fusion.2), channel_id=1, source_target_pairs={{0,1},{1,0},{2,3},{3,2},{4,5},{5,4},{6,7},{7,6},{8,9},{9,8},{10,11... | collective-permute-start | bytes 835592 | tf_op jit(solution)/shard_map/ppermute | solution.py:79
  98.4 6.4 %collective-permute-start.14 = (bf16[128,320]{1,0:T(8,128)(2,1)S(1)}, bf16[128,320]{1,0:T(8,128)(2,1)S(1)}, u32[]{:S(2)}, u32[]{:S(2)}) collective-permute-start(bf16[128,320]{1,0:T(8,128)(2,1)S(1)} %get-tuple-element.193), channel_id=1, source_target_pairs={{0,2},{1,3},{2,0},{3,1},{4,6},{5,7},{6,4},{7,5},{8,10},{9,11},{10,... | collective-permute-start | bytes 245768 | tf_op jit(solution)/shard_map/ppermute | solution.py:79
  99.4 6.6 %collective-permute-start.13 = (bf16[128,320]{1,0:T(8,128)(2,1)S(1)}, bf16[128,320]{1,0:T(8,128)(2,1)S(1)}, u32[]{:S(2)}, u32[]{:S(2)}) collective-permute-start(bf16[128,320]{1,0:T(8,128)(2,1)S(1)} %get-tuple-element.194), channel_id=1, source_target_pairs={{0,3},{1,2},{2,1},{3,0},{4,7},{5,6},{6,5},{7,4},{8,11},{9,10},{10,... | collective-permute-start | bytes 245768 | tf_op jit(solution)/shard_map/ppermute | solution.py:79
  111.3 10.6 %collective-permute-start.21 = (bf16[128,1088]{0,1:T(8,128)(2,1)S(1)}, bf16[128,1088]{0,1:T(8,128)(2,1)}, u32[]{:S(2)}, u32[]{:S(2)}) collective-permute-start(bf16[128,1088]{0,1:T(8,128)(2,1)S(1)} %add_convert_fusion.1), channel_id=1, source_target_pairs={{0,3},{1,2},{2,1},{3,0},{4,7},{5,6},{6,5},{7,4},{8,11},{9,10},{10,... | collective-permute-start | bytes 835592 | tf_op jit(solution)/shard_map/ppermute | solution.py:79
  112.9 15.1 %collective-permute-start.20 = (bf16[128,1088]{0,1:T(8,128)(2,1)S(1)}, bf16[128,1088]{0,1:T(8,128)(2,1)}, u32[]{:S(2)}, u32[]{:S(2)}) collective-permute-start(bf16[128,1088]{0,1:T(8,128)(2,1)S(1)} %add_convert_fusion.1), channel_id=1, source_target_pairs={{0,2},{1,3},{2,0},{3,1},{4,6},{5,7},{6,4},{7,5},{8,10},{9,11},{10,... | collective-permute-start | bytes 835592 | tf_op jit(solution)/shard_map/ppermute | solution.py:79
  113.8 15.7 %collective-permute-start.19 = (bf16[128,1088]{0,1:T(8,128)(2,1)S(1)}, bf16[128,1088]{0,1:T(8,128)(2,1)}, u32[]{:S(2)}, u32[]{:S(2)}) collective-permute-start(bf16[128,1088]{0,1:T(8,128)(2,1)S(1)} %add_convert_fusion.1), channel_id=1, source_target_pairs={{0,1},{1,0},{2,3},{3,2},{4,5},{5,4},{6,7},{7,6},{8,9},{9,8},{10,11... | collective-permute-start | bytes 835592 | tf_op jit(solution)/shard_map/ppermute | solution.py:79
  115.2 20.2 %collective-permute-start.33 = (bf16[128,1088]{0,1:T(8,128)(2,1)S(1)}, bf16[128,1088]{0,1:T(8,128)(2,1)}, u32[]{:S(2)}, u32[]{:S(2)}) collective-permute-start(bf16[128,1088]{0,1:T(8,128)(2,1)S(1)} %get-tuple-element.167), channel_id=1, source_target_pairs={{0,3},{1,2},{2,1},{3,0},{4,7},{5,6},{6,5},{7,4},{8,11},{9,10},{10,... | collective-permute-start | bytes 835592 | tf_op jit(solution)/shard_map/ppermute | solution.py:79
  116.9 23.0 %collective-permute-start.32 = (bf16[128,1088]{0,1:T(8,128)(2,1)S(1)}, bf16[128,1088]{0,1:T(8,128)(2,1)}, u32[]{:S(2)}, u32[]{:S(2)}) collective-permute-start(bf16[128,1088]{0,1:T(8,128)(2,1)S(1)} %get-tuple-element.167), channel_id=1, source_target_pairs={{0,2},{1,3},{2,0},{3,1},{4,6},{5,7},{6,4},{7,5},{8,10},{9,11},{10,... | collective-permute-start | bytes 835592 | tf_op jit(solution)/shard_map/ppermute | solution.py:79
  121.9 18.0 %collective-permute-start.31 = (bf16[128,1088]{0,1:T(8,128)(2,1)S(1)}, bf16[128,1088]{0,1:T(8,128)(2,1)S(1)}, u32[]{:S(2)}, u32[]{:S(2)}) collective-permute-start(bf16[128,1088]{0,1:T(8,128)(2,1)S(1)} %get-tuple-element.167), channel_id=1, source_target_pairs={{0,1},{1,0},{2,3},{3,2},{4,5},{5,4},{6,7},{7,6},{8,9},{9,8},{10,11... | collective-permute-start | bytes 835592 | tf_op jit(solution)/shard_map/ppermute | solution.py:79
  127.9 81.1 %collective-permute-start.62 = (bf16[128,1088]{1,0:T(8,128)(2,1)S(1)}, bf16[128,1088]{1,0:T(8,128)(2,1)}, u32[]{:S(2)}, u32[]{:S(2)}) collective-permute-start(bf16[128,1088]{1,0:T(8,128)(2,1)S(1)} %slice.643), channel_id=1, source_target_pairs={{0,3},{1,2},{2,1},{3,0},{4,7},{5,6},{6,5},{7,4},{8,11},{9,10},{10,... | collective-permute-start | bytes 835592 | tf_op jit(solution)/shard_map/ppermute | solution.py:79
  129.5 81.9 %collective-permute-start.61 = (bf16[128,1088]{1,0:T(8,128)(2,1)S(1)}, bf16[128,1088]{1,0:T(8,128)(2,1)}, u32[]{:S(2)}, u32[]{:S(2)}) collective-permute-start(bf16[128,1088]{1,0:T(8,128)(2,1)S(1)} %slice.643), channel_id=1, source_target_pairs={{0,2},{1,3},{2,0},{3,1},{4,6},{5,7},{6,4},{7,5},{8,10},{9,11},{10,... | collective-permute-start | bytes 835592 | tf_op jit(solution)/shard_map/ppermute | solution.py:79
  164.3 21.0 %collective-permute-start.36 = (bf16[128,1088]{0,1:T(8,128)(2,1)}, bf16[128,1088]{0,1:T(8,128)(2,1)}, u32[]{:S(2)}, u32[]{:S(2)}) collective-permute-start(bf16[128,1088]{0,1:T(8,128)(2,1)} %get-tuple-element.149), channel_id=1, source_target_pairs={{0,3},{1,2},{2,1},{3,0},{4,7},{5,6},{6,5},{7,4},{8,11},{9,10},{10,... | collective-permute-start | bytes 835592 | tf_op jit(solution)/shard_map/ppermute | solution.py:79
  166.7 21.1 %collective-permute-start.35 = (bf16[128,1088]{0,1:T(8,128)(2,1)S(1)}, bf16[128,1088]{0,1:T(8,128)(2,1)}, u32[]{:S(2)}, u32[]{:S(2)}) collective-permute-start(bf16[128,1088]{0,1:T(8,128)(2,1)S(1)} %get-tuple-element.150), channel_id=1, source_target_pairs={{0,2},{1,3},{2,0},{3,1},{4,6},{5,7},{6,4},{7,5},{8,10},{9,11},{10,... | collective-permute-start | bytes 835592 | tf_op jit(solution)/shard_map/ppermute | solution.py:79
  167.3 21.1 %collective-permute-start.34 = (bf16[128,1088]{0,1:T(8,128)(2,1)S(1)}, bf16[128,1088]{0,1:T(8,128)(2,1)}, u32[]{:S(2)}, u32[]{:S(2)}) collective-permute-start(bf16[128,1088]{0,1:T(8,128)(2,1)S(1)} %get-tuple-element.148), channel_id=1, source_target_pairs={{0,1},{1,0},{2,3},{3,2},{4,5},{5,4},{6,7},{7,6},{8,9},{9,8},{10,11... | collective-permute-start | bytes 835592 | tf_op jit(solution)/shard_map/ppermute | solution.py:79
  185.3 10.7 %collective-permute-start.30 = (bf16[128,1088]{0,1:T(8,128)(2,1)}, bf16[128,1088]{0,1:T(8,128)(2,1)S(1)}, u32[]{:S(2)}, u32[]{:S(2)}) collective-permute-start(bf16[128,1088]{0,1:T(8,128)(2,1)} %get-tuple-element.152), channel_id=1, source_target_pairs={{0,3},{1,2},{2,1},{3,0},{4,7},{5,6},{6,5},{7,4},{8,11},{9,10},{10,... | collective-permute-start | bytes 835592 | tf_op jit(solution)/shard_map/ppermute | solution.py:79
  187.8 12.7 %collective-permute-start.29 = (bf16[128,1088]{0,1:T(8,128)(2,1)S(1)}, bf16[128,1088]{0,1:T(8,128)(2,1)S(1)}, u32[]{:S(2)}, u32[]{:S(2)}) collective-permute-start(bf16[128,1088]{0,1:T(8,128)(2,1)S(1)} %get-tuple-element.153), channel_id=1, source_target_pairs={{0,2},{1,3},{2,0},{3,1},{4,6},{5,7},{6,4},{7,5},{8,10},{9,11},{10,... | collective-permute-start | bytes 835592 | tf_op jit(solution)/shard_map/ppermute | solution.py:79
  188.3 13.7 %collective-permute-start.28 = (bf16[128,1088]{0,1:T(8,128)(2,1)S(1)}, bf16[128,1088]{0,1:T(8,128)(2,1)S(1)}, u32[]{:S(2)}, u32[]{:S(2)}) collective-permute-start(bf16[128,1088]{0,1:T(8,128)(2,1)S(1)} %get-tuple-element.151), channel_id=1, source_target_pairs={{0,1},{1,0},{2,3},{3,2},{4,5},{5,4},{6,7},{7,6},{8,9},{9,8},{10,11... | collective-permute-start | bytes 835592 | tf_op jit(solution)/shard_map/ppermute | solution.py:79
  196.1 15.3 %collective-permute-start.60 = (bf16[128,1088]{1,0:T(8,128)(2,1)S(1)}, bf16[128,1088]{1,0:T(8,128)(2,1)}, u32[]{:S(2)}, u32[]{:S(2)}) collective-permute-start(bf16[128,1088]{1,0:T(8,128)(2,1)S(1)} %slice.643), channel_id=1, source_target_pairs={{0,1},{1,0},{2,3},{3,2},{4,5},{5,4},{6,7},{7,6},{8,9},{9,8},{10,11... | collective-permute-start | bytes 835592 | tf_op jit(solution)/shard_map/ppermute | solution.py:79
  205.2 7.8 %collective-permute-start.65 = (bf16[128,272]{0,1:T(8,128)(2,1)}, bf16[128,272]{0,1:T(8,128)(2,1)}, u32[]{:S(2)}, u32[]{:S(2)}) collective-permute-start(bf16[128,272]{0,1:T(8,128)(2,1)} %get-tuple-element.222), channel_id=1, source_target_pairs={{0,3},{1,2},{2,1},{3,0},{4,7},{5,6},{6,5},{7,4},{8,11},{9,10},{10,... | collective-permute-start | bytes 208904 | tf_op jit(solution)/shard_map/ppermute | solution.py:79
  206.7 7.7 %collective-permute-start.64 = (bf16[128,272]{0,1:T(8,128)(2,1)}, bf16[128,272]{0,1:T(8,128)(2,1)}, u32[]{:S(2)}, u32[]{:S(2)}) collective-permute-start(bf16[128,272]{0,1:T(8,128)(2,1)} %get-tuple-element.224), channel_id=1, source_target_pairs={{0,2},{1,3},{2,0},{3,1},{4,6},{5,7},{6,4},{7,5},{8,10},{9,11},{10,... | collective-permute-start | bytes 208904 | tf_op jit(solution)/shard_map/ppermute | solution.py:79
  209.1 5.9 %collective-permute-start.63 = (bf16[128,272]{0,1:T(8,128)(2,1)}, bf16[128,272]{0,1:T(8,128)(2,1)}, u32[]{:S(2)}, u32[]{:S(2)}) collective-permute-start(bf16[128,272]{0,1:T(8,128)(2,1)} %get-tuple-element.223), channel_id=1, source_target_pairs={{0,1},{1,0},{2,3},{3,2},{4,5},{5,4},{6,7},{7,6},{8,9},{9,8},{10,11... | collective-permute-start | bytes 208904 | tf_op jit(solution)/shard_map/ppermute | solution.py:79
  211.4 68.2 %collective-permute-start.70 = (bf16[4,136,1088]{2,1,0:T(8,128)(2,1)}, bf16[4,136,1088]{2,1,0:T(8,128)(2,1)S(1)}, u32[]{:S(2)}, u32[]{:S(2)}) collective-permute-start(bf16[4,136,1088]{2,1,0:T(8,128)(2,1)} %fusion.17), channel_id=1, source_target_pairs={{0,4},{4,0},{8,12},{12,8},{16,20},{20,16},{24,28},{28,24},{1,5},{5... | collective-permute-start | bytes 3551240 | tf_op jit(solution)/shard_map/ppermute | solution.py:79
  211.4 7.6 %collective-permute-start.39 = (bf16[128,320]{1,0:T(8,128)(2,1)S(1)}, bf16[128,320]{1,0:T(8,128)(2,1)S(1)}, u32[]{:S(2)}, u32[]{:S(2)}) collective-permute-start(bf16[128,320]{1,0:T(8,128)(2,1)S(1)} %get-tuple-element.220), channel_id=1, source_target_pairs={{0,3},{1,2},{2,1},{3,0},{4,7},{5,6},{6,5},{7,4},{8,11},{9,10},{10,... | collective-permute-start | bytes 245768 | tf_op jit(solution)/shard_map/ppermute | solution.py:79
  213.0 6.7 %collective-permute-start.38 = (bf16[128,320]{1,0:T(8,128)(2,1)S(1)}, bf16[128,320]{1,0:T(8,128)(2,1)S(1)}, u32[]{:S(2)}, u32[]{:S(2)}) collective-permute-start(bf16[128,320]{1,0:T(8,128)(2,1)S(1)} %get-tuple-element.219), channel_id=1, source_target_pairs={{0,2},{1,3},{2,0},{3,1},{4,6},{5,7},{6,4},{7,5},{8,10},{9,11},{10,... | collective-permute-start | bytes 245768 | tf_op jit(solution)/shard_map/ppermute | solution.py:79
  219.0 37.2 %collective-permute-start.66 = (bf16[4,136,272]{2,1,0:T(8,128)(2,1)}, bf16[4,136,272]{2,1,0:T(8,128)(2,1)}, u32[]{:S(2)}, u32[]{:S(2)}) collective-permute-start(bf16[4,136,272]{2,1,0:T(8,128)(2,1)} %fusion.54), channel_id=1, source_target_pairs={{0,4},{4,0},{8,12},{12,8},{16,20},{20,16},{24,28},{28,24},{1,5},{5... | collective-permute-start | bytes 887816 | tf_op jit(solution)/shard_map/ppermute | solution.py:79
  233.4 10.6 %collective-permute-start.42 = (bf16[128,1088]{0,1:T(8,128)(2,1)S(1)}, bf16[128,1088]{0,1:T(8,128)(2,1)}, u32[]{:S(2)}, u32[]{:S(2)}) collective-permute-start(bf16[128,1088]{0,1:T(8,128)(2,1)S(1)} %get-tuple-element.146), channel_id=1, source_target_pairs={{0,3},{1,2},{2,1},{3,0},{4,7},{5,6},{6,5},{7,4},{8,11},{9,10},{10,... | collective-permute-start | bytes 835592 | tf_op jit(solution)/shard_map/ppermute | solution.py:79
  234.9 14.1 %collective-permute-start.41 = (bf16[128,1088]{0,1:T(8,128)(2,1)S(1)}, bf16[128,1088]{0,1:T(8,128)(2,1)}, u32[]{:S(2)}, u32[]{:S(2)}) collective-permute-start(bf16[128,1088]{0,1:T(8,128)(2,1)S(1)} %get-tuple-element.147), channel_id=1, source_target_pairs={{0,2},{1,3},{2,0},{3,1},{4,6},{5,7},{6,4},{7,5},{8,10},{9,11},{10,... | collective-permute-start | bytes 835592 | tf_op jit(solution)/shard_map/ppermute | solution.py:79
  235.8 13.3 %collective-permute-start.40 = (bf16[128,1088]{0,1:T(8,128)(2,1)S(1)}, bf16[128,1088]{0,1:T(8,128)(2,1)}, u32[]{:S(2)}, u32[]{:S(2)}) collective-permute-start(bf16[128,1088]{0,1:T(8,128)(2,1)S(1)} %get-tuple-element.145), channel_id=1, source_target_pairs={{0,1},{1,0},{2,3},{3,2},{4,5},{5,4},{6,7},{7,6},{8,9},{9,8},{10,11... | collective-permute-start | bytes 835592 | tf_op jit(solution)/shard_map/ppermute | solution.py:79
  251.6 7.4 %collective-permute-start.49 = (f32[1632]{0:T(1024)S(1)}, f32[1632]{0:T(1024)S(1)}, u32[]{:S(2)}, u32[]{:S(2)}) collective-permute-start(f32[1632]{0:T(1024)S(1)} %get-tuple-element.87), channel_id=1, source_target_pairs={{0,28},{4,24},{8,20},{12,16},{16,12},{20,8},{24,4},{28,0},{1,29},{... | collective-permute-start | bytes 19592 | tf_op jit(solution)/shard_map/ppermute | solution.py:79
  253.0 6.1 %collective-permute-start.48 = (f32[1632]{0:T(1024)S(1)}, f32[1632]{0:T(1024)S(1)}, u32[]{:S(2)}, u32[]{:S(2)}) collective-permute-start(f32[1632]{0:T(1024)S(1)} %get-tuple-element.91), channel_id=1, source_target_pairs={{0,24},{4,28},{8,16},{12,20},{16,8},{20,12},{24,0},{28,4},{1,25},{... | collective-permute-start | bytes 19592 | tf_op jit(solution)/shard_map/ppermute | solution.py:79
  256.3 6.3 %collective-permute-start.46 = (f32[1632]{0:T(1024)S(1)}, f32[1632]{0:T(1024)S(1)}, u32[]{:S(2)}, u32[]{:S(2)}) collective-permute-start(f32[1632]{0:T(1024)S(1)} %get-tuple-element.90), channel_id=1, source_target_pairs={{0,16},{4,20},{8,24},{12,28},{16,0},{20,4},{24,8},{28,12},{1,17},{... | collective-permute-start | bytes 19592 | tf_op jit(solution)/shard_map/ppermute | solution.py:79
  262.5 24.9 %collective-permute-start.77 = (bf16[4,136,1088]{2,1,0:T(8,128)(2,1)S(1)}, bf16[4,136,1088]{2,1,0:T(8,128)(2,1)S(1)}, u32[]{:S(2)}, u32[]{:S(2)}) collective-permute-start(bf16[4,136,1088]{2,1,0:T(8,128)(2,1)S(1)} %copy-done.9), channel_id=1, source_target_pairs={{0,4},{4,0},{8,12},{12,8},{16,20},{20,16},{24,28},{28,24},{1,5},{5... | collective-permute-start | bytes 3551240 | tf_op jit(solution)/shard_map/ppermute | solution.py:79
  267.5 7.6 %collective-permute-start.69 = (bf16[136,272]{1,0:T(8,128)(2,1)S(1)}, bf16[136,272]{1,0:T(8,128)(2,1)S(1)}, u32[]{:S(2)}, u32[]{:S(2)}) collective-permute-start(bf16[136,272]{1,0:T(8,128)(2,1)S(1)} %get-tuple-element.159), channel_id=1, source_target_pairs={{0,24},{4,28},{8,16},{12,20},{16,8},{20,12},{24,0},{28,4},{1,25},{... | collective-permute-start | bytes 221960 | tf_op jit(solution)/shard_map/ppermute | solution.py:79
  269.2 9.7 %collective-permute-start.68 = (bf16[136,272]{1,0:T(8,128)(2,1)S(1)}, bf16[136,272]{1,0:T(8,128)(2,1)S(1)}, u32[]{:S(2)}, u32[]{:S(2)}) collective-permute-start(bf16[136,272]{1,0:T(8,128)(2,1)S(1)} %get-tuple-element.158), channel_id=1, source_target_pairs={{0,16},{4,20},{8,24},{12,28},{16,0},{20,4},{24,8},{28,12},{1,17},{... | collective-permute-start | bytes 221960 | tf_op jit(solution)/shard_map/ppermute | solution.py:79
  270.4 8.4 %collective-permute-start.67 = (bf16[136,272]{1,0:T(8,128)(2,1)S(1)}, bf16[136,272]{1,0:T(8,128)(2,1)S(1)}, u32[]{:S(2)}, u32[]{:S(2)}) collective-permute-start(bf16[136,272]{1,0:T(8,128)(2,1)S(1)} %get-tuple-element.157), channel_id=1, source_target_pairs={{0,8},{4,12},{8,0},{12,4},{16,24},{20,28},{24,16},{28,20},{1,9},{5... | collective-permute-start | bytes 221960 | tf_op jit(solution)/shard_map/ppermute | solution.py:79
  275.2 14.4 %collective-permute-start.53 = (bf16[4,136,960]{2,1,0:T(8,128)(2,1)S(1)}, bf16[4,136,960]{2,1,0:T(8,128)(2,1)S(1)}, u32[]{:S(2)}, u32[]{:S(2)}) collective-permute-start(bf16[4,136,960]{2,1,0:T(8,128)(2,1)S(1)} %copy-done.10), channel_id=1, source_target_pairs={{0,4},{4,0},{8,12},{12,8},{16,20},{20,16},{24,28},{28,24},{1,5},{5... | collective-permute-start | bytes 3133448 | tf_op jit(solution)/shard_map/ppermute | solution.py:79
  283.0 12.2 %collective-permute-start.73 = (bf16[136,1088]{1,0:T(8,128)(2,1)S(1)}, bf16[136,1088]{1,0:T(8,128)(2,1)S(1)}, u32[]{:S(2)}, u32[]{:S(2)}) collective-permute-start(bf16[136,1088]{1,0:T(8,128)(2,1)S(1)} %get-tuple-element.141), channel_id=1, source_target_pairs={{0,24},{4,28},{8,16},{12,20},{16,8},{20,12},{24,0},{28,4},{1,25},{... | collective-permute-start | bytes 887816 | tf_op jit(solution)/shard_map/ppermute | solution.py:79
  284.7 41.1 %collective-permute-start.72 = (bf16[136,1088]{1,0:T(8,128)(2,1)S(1)}, bf16[136,1088]{1,0:T(8,128)(2,1)S(1)}, u32[]{:S(2)}, u32[]{:S(2)}) collective-permute-start(bf16[136,1088]{1,0:T(8,128)(2,1)S(1)} %get-tuple-element.140), channel_id=1, source_target_pairs={{0,16},{4,20},{8,24},{12,28},{16,0},{20,4},{24,8},{28,12},{1,17},{... | collective-permute-start | bytes 887816 | tf_op jit(solution)/shard_map/ppermute | solution.py:79
  284.7 42.8 %collective-permute-start.71 = (bf16[136,1088]{1,0:T(8,128)(2,1)S(1)}, bf16[136,1088]{1,0:T(8,128)(2,1)S(1)}, u32[]{:S(2)}, u32[]{:S(2)}) collective-permute-start(bf16[136,1088]{1,0:T(8,128)(2,1)S(1)} %get-tuple-element.139), channel_id=1, source_target_pairs={{0,8},{4,12},{8,0},{12,4},{16,24},{20,28},{24,16},{28,20},{1,9},{5... | collective-permute-start | bytes 887816 | tf_op jit(solution)/shard_map/ppermute | solution.py:79
  287.9 39.9 %collective-permute-start.80 = (bf16[136,1088]{1,0:T(8,128)(2,1)S(1)}, bf16[136,1088]{1,0:T(8,128)(2,1)S(1)}, u32[]{:S(2)}, u32[]{:S(2)}) collective-permute-start(bf16[136,1088]{1,0:T(8,128)(2,1)S(1)} %get-tuple-element.138), channel_id=1, source_target_pairs={{0,24},{4,28},{8,16},{12,20},{16,8},{20,12},{24,0},{28,4},{1,25},{... | collective-permute-start | bytes 887816 | tf_op jit(solution)/shard_map/ppermute | solution.py:79
  289.6 61.6 %collective-permute-start.79 = (bf16[136,1088]{1,0:T(8,128)(2,1)S(1)}, bf16[136,1088]{1,0:T(8,128)(2,1)S(1)}, u32[]{:S(2)}, u32[]{:S(2)}) collective-permute-start(bf16[136,1088]{1,0:T(8,128)(2,1)S(1)} %get-tuple-element.137), channel_id=1, source_target_pairs={{0,16},{4,20},{8,24},{12,28},{16,0},{20,4},{24,8},{28,12},{1,17},{... | collective-permute-start | bytes 887816 | tf_op jit(solution)/shard_map/ppermute | solution.py:79
  295.2 56.6 %collective-permute-start.78 = (bf16[136,1088]{1,0:T(8,128)(2,1)S(1)}, bf16[136,1088]{1,0:T(8,128)(2,1)S(1)}, u32[]{:S(2)}, u32[]{:S(2)}) collective-permute-start(bf16[136,1088]{1,0:T(8,128)(2,1)S(1)} %get-tuple-element.136), channel_id=1, source_target_pairs={{0,8},{4,12},{8,0},{12,4},{16,24},{20,28},{24,16},{28,20},{1,9},{5... | collective-permute-start | bytes 887816 | tf_op jit(solution)/shard_map/ppermute | solution.py:79
  325.8 42.5 %collective-permute-start.56 = (bf16[136,960]{1,0:T(8,128)(2,1)}, bf16[136,960]{1,0:T(8,128)(2,1)}, u32[]{:S(2)}, u32[]{:S(2)}) collective-permute-start(bf16[136,960]{1,0:T(8,128)(2,1)} %get-tuple-element.144), channel_id=1, source_target_pairs={{0,24},{4,28},{8,16},{12,20},{16,8},{20,12},{24,0},{28,4},{1,25},{... | collective-permute-start | bytes 783368 | tf_op jit(solution)/shard_map/ppermute | solution.py:79
  327.4 40.9 %collective-permute-start.55 = (bf16[136,960]{1,0:T(8,128)(2,1)}, bf16[136,960]{1,0:T(8,128)(2,1)}, u32[]{:S(2)}, u32[]{:S(2)}) collective-permute-start(bf16[136,960]{1,0:T(8,128)(2,1)} %get-tuple-element.143), channel_id=1, source_target_pairs={{0,16},{4,20},{8,24},{12,28},{16,0},{20,4},{24,8},{28,12},{1,17},{... | collective-permute-start | bytes 783368 | tf_op jit(solution)/shard_map/ppermute | solution.py:79
  327.9 26.5 %collective-permute-start.74 = (bf16[136,272]{1,0:T(8,128)(2,1)S(1)}, bf16[136,272]{1,0:T(8,128)(2,1)S(1)}, u32[]{:S(2)}, u32[]{:S(2)}) collective-permute-start(bf16[136,272]{1,0:T(8,128)(2,1)S(1)} %get-tuple-element.213), channel_id=1, source_target_pairs={{0,3},{1,2},{2,1},{3,0},{4,7},{5,6},{6,5},{7,4},{8,11},{9,10},{10,... | collective-permute-start | bytes 221960 | tf_op jit(solution)/shard_map/ppermute | solution.py:79
  354.3 14.0 %collective-permute-start.54 = (bf16[136,960]{1,0:T(8,128)(2,1)S(1)}, bf16[136,960]{1,0:T(8,128)(2,1)}, u32[]{:S(2)}, u32[]{:S(2)}) collective-permute-start(bf16[136,960]{1,0:T(8,128)(2,1)S(1)} %get-tuple-element.142), channel_id=1, source_target_pairs={{0,8},{4,12},{8,0},{12,4},{16,24},{20,28},{24,16},{28,20},{1,9},{5... | collective-permute-start | bytes 783368 | tf_op jit(solution)/shard_map/ppermute | solution.py:79
  355.9 6.0 %collective-permute-start.81 = (bf16[136,272]{1,0:T(8,128)(2,1)}, bf16[136,272]{1,0:T(8,128)(2,1)}, u32[]{:S(2)}, u32[]{:S(2)}) collective-permute-start(bf16[136,272]{1,0:T(8,128)(2,1)} %get-tuple-element.208), channel_id=1, source_target_pairs={{0,3},{1,2},{2,1},{3,0},{4,7},{5,6},{6,5},{7,4},{8,11},{9,10},{10,... | collective-permute-start | bytes 221960 | tf_op jit(solution)/shard_map/ppermute | solution.py:79
  357.3 10.0 %collective-permute-start.82 = (bf16[136,272]{1,0:T(8,128)(2,1)}, bf16[136,272]{1,0:T(8,128)(2,1)}, u32[]{:S(2)}, u32[]{:S(2)}) collective-permute-start(bf16[136,272]{1,0:T(8,128)(2,1)} %get-tuple-element.209), channel_id=1, source_target_pairs={{0,2},{1,3},{2,0},{3,1},{4,6},{5,7},{6,4},{7,5},{8,10},{9,11},{10,... | collective-permute-start | bytes 221960 | tf_op jit(solution)/shard_map/ppermute | solution.py:79
  (74 other events, 610.6 us)
Sparse Core Ops, SparseCore 0:
  21.8 30.3 all-gather.4
  54.4 32.3 all-gather.6
  89.0 31.8 all-gather.8
  123.0 31.9 all-gather.10
